TPU v7x, 32 devices: a whole 2x2x4 slice. The times are simulated.
32 devices in a mesh: tile: 2 (over y), date: 4 (over z), rng: 2 (over x), az: 2 (over core).
Axes of the slice: x: 2, y: 2, z: 4, core: 2. Of those that a mesh axis runs over, the one named last changes fastest.
Arguments:
- acquisitions: bfloat16 [32, 256, 2, 512], P(('tile', 'date'), 'az', None, 'rng'), parts along dimension 0, may hold values from -80 to 80
- date_pairs: int32 [2, 32], P(None, ('date', 'rng', 'az')), may hold values from 0 to 15, as said below
Outputs:
- filtered: bfloat16 [64, 2, 64, 32], P(('tile', 'date', 'rng', 'az')), parts along dimension 0
- coherence: bfloat16 [64, 64, 32], P(('tile', 'date', 'rng', 'az')), parts along dimension 0
There are 2 independent parts, one for each index of `tile`. A program takes and returns all parts, laid end to end along the dimension named above; an argument that names none is the same for every part. Nothing has to cross between parts.
Inputs may be any that keep to these rules, and one draw needn't show every extreme that they name: For every column p, date_pairs[0,p] < date_pairs[1,p] <= date_pairs[0,p] + 8; some dates appear in many more pairs than others.
All inputs are finite; a program needn't handle non-finite values.
Results may differ from a plain program's by a relative error of at most 0.001.
Values may be sent and summed in bfloat16 or wider, within the bound.
No kernel may reach another device: no remote copies, remote signals or barrier semaphores. Data moves between devices by JAX's collectives and lax.ppermute only.
A program may use at most 64 MiB of HBM per device.

v0:
```python
import math

import jax
import jax.numpy as jnp
import numpy as np
from jax import lax
from jax.experimental import pallas as pl
from jax.experimental.pallas import tpu as pltpu
from jax.sharding import PartitionSpec as P


PATCH = 64
LOOK_AZ = 4
LOOK_RG = 16
HALF = 32
LANES = 128


EPSILON = 1e-06
HIGHEST = lax.Precision.HIGHEST


def fourier_tables(length):
    position = jnp.arange(length, dtype=jnp.int32)
    product = position[:, None] * position[None, :] % length
    angle = product.astype(jnp.float32) * (2.0 * math.pi / length)
    return (jnp.cos(angle), jnp.sin(angle))


def taper_window(length):
    midway = length // 2
    position = jnp.arange(length, dtype=jnp.float32)
    ramp_line = 1.0 - jnp.abs(position + 0.5 - midway) / midway
    return ramp_line[:, None] * ramp_line[None, :]


def transform(real_part, imag_part, cosine_table, sine_table, inverse):
    length = cosine_table.shape[0]
    if inverse:
        matrix = jnp.concatenate(
            [
                jnp.concatenate([cosine_table, sine_table], 1),
                jnp.concatenate([-sine_table, cosine_table], 1),
            ],
            0,
        )
    else:
        matrix = jnp.concatenate(
            [
                jnp.concatenate([cosine_table, -sine_table], 1),
                jnp.concatenate([sine_table, cosine_table], 1),
            ],
            0,
        )
    joined = jnp.concatenate([real_part, imag_part], axis=-1)
    across = jnp.einsum("bnc,cd->bnd", joined, matrix, precision=HIGHEST)
    rotated = jnp.einsum(
        "tkn,bnd->btkd", jnp.stack([cosine_table, sine_table]), across, precision=HIGHEST
    )
    with_cosine = rotated[:, 0]
    with_sine = rotated[:, 1]
    if inverse:
        scaling = 1.0 / (length * length)
        out_real = (with_cosine[..., :length] - with_sine[..., length:]) * scaling
        out_imag = (with_cosine[..., length:] + with_sine[..., :length]) * scaling
    else:
        out_real = with_cosine[..., :length] + with_sine[..., length:]
        out_imag = with_cosine[..., length:] - with_sine[..., :length]
    return (out_real, out_imag)


def goldstein(
    extended_real, extended_imag, cosine_table, sine_table, window, block_lines, block_samples
):
    groups = extended_real.shape[0]
    extent_line = extended_real.shape[1]
    extent_sample = extended_real.shape[2]
    length = cosine_table.shape[0]
    midway = length // 2
    summed_real = jnp.zeros_like(extended_real)
    summed_imag = jnp.zeros_like(extended_imag)
    for start_line in (0, midway):
        for start_sample in (0, midway):
            count_line = (extent_line - start_line) // length
            count_sample = (extent_sample - start_sample) // length
            stop_line = start_line + count_line * length
            stop_sample = start_sample + count_sample * length

            def extract(values):
                region = values[:, start_line:stop_line, start_sample:stop_sample]
                region = region.reshape(groups, count_line, length, count_sample, length)
                return region.transpose(0, 1, 3, 2, 4).reshape(-1, length, length)

            def insert(values):
                shaped = (values * window).reshape(groups, count_line, count_sample, length, length)
                return shaped.transpose(0, 1, 3, 2, 4).reshape(
                    groups, count_line * length, count_sample * length
                )

            spec_real, spec_imag = transform(
                extract(extended_real), extract(extended_imag), cosine_table, sine_table, False
            )
            energy = spec_real * spec_real + spec_imag * spec_imag
            weight = (energy + 1.0) ** 0.25
            weight = weight / jnp.mean(weight, axis=(1, 2), keepdims=True)
            back_real, back_imag = transform(
                spec_real * weight, spec_imag * weight, cosine_table, sine_table, True
            )
            summed_real = summed_real.at[:, start_line:stop_line, start_sample:stop_sample].add(
                insert(back_real)
            )
            summed_imag = summed_imag.at[:, start_line:stop_line, start_sample:stop_sample].add(
                insert(back_imag)
            )
    center_real = summed_real[:, midway : midway + block_lines, midway : midway + block_samples]
    center_imag = summed_imag[:, midway : midway + block_lines, midway : midway + block_samples]
    return (center_real, center_imag)


def local(acquisitions, date_pairs):
    every_pair = lax.all_gather(date_pairs, ("date", "rng", "az"), axis=1, tiled=True)
    by_lines = lax.all_to_all(acquisitions, "date", split_axis=1, concat_axis=0, tiled=True)
    line_count = by_lines.shape[1]
    sample_count = by_lines.shape[3]
    look_lines = line_count // LOOK_AZ
    look_samples = sample_count // LOOK_RG

    def take_looks(values):
        leading = values.shape[:-2]
        shaped = values.reshape(leading + (look_lines, LOOK_AZ, look_samples, LOOK_RG))
        return jnp.sum(shaped, axis=(-3, -1)) * (1.0 / (LOOK_AZ * LOOK_RG))

    real_lines = by_lines[:, :, 0, :].astype(jnp.float32)
    imag_lines = by_lines[:, :, 1, :].astype(jnp.float32)
    intensity = take_looks(real_lines * real_lines + imag_lines * imag_lines)
    pair_total = every_pair.shape[1]
    block_rows = math.gcd(pair_total, 32)
    turns = pair_total // block_rows
    earlier = every_pair[0].reshape(turns, block_rows)
    later = every_pair[1].reshape(turns, block_rows)

    def cross_block(indices):
        left = jnp.take(by_lines, indices[0], axis=0).astype(jnp.float32)
        right = jnp.take(by_lines, indices[1], axis=0).astype(jnp.float32)
        cross_real = take_looks(left[:, :, 0] * right[:, :, 0] + left[:, :, 1] * right[:, :, 1])
        cross_imag = take_looks(left[:, :, 1] * right[:, :, 0] - left[:, :, 0] * right[:, :, 1])
        return (cross_real, cross_imag)

    cross_real, cross_imag = lax.map(cross_block, (earlier, later))
    cross_real = cross_real.reshape(pair_total, look_lines, look_samples)
    cross_imag = cross_imag.reshape(pair_total, look_lines, look_samples)
    power_early = jnp.take(intensity, every_pair[0], axis=0)
    power_late = jnp.take(intensity, every_pair[1], axis=0)
    denominator = jnp.sqrt((power_early + EPSILON) * (power_late + EPSILON))
    payload = jnp.stack([cross_real / denominator, cross_imag / denominator], axis=1)
    partway = lax.all_to_all(
        lax.all_to_all(payload, "date", split_axis=0, concat_axis=2, tiled=True),
        "rng",
        split_axis=0,
        concat_axis=3,
        tiled=True,
    )
    returned = lax.all_to_all(partway, "az", split_axis=0, concat_axis=2, tiled=True)
    ratio_real = returned[:, 0]
    ratio_imag = returned[:, 1]
    coherence = jnp.sqrt(ratio_real * ratio_real + ratio_imag * ratio_imag).astype(jnp.bfloat16)
    block_lines = ratio_real.shape[1]
    block_samples = ratio_real.shape[2]
    padding = ((0, 0), (HALF, HALF), (HALF, HALF))
    extended_real = jnp.pad(ratio_real, padding)
    extended_imag = jnp.pad(ratio_imag, padding)
    cosine_table, sine_table = fourier_tables(PATCH)
    window = taper_window(PATCH)
    out_real, out_imag = goldstein(
        extended_real, extended_imag, cosine_table, sine_table, window, block_lines, block_samples
    )
    filtered = jnp.stack([out_real, out_imag], axis=1).astype(jnp.bfloat16)
    return (filtered, coherence)


def rounded_parts(values):
    high = values.astype(jnp.bfloat16)
    low = (values - high.astype(jnp.float32)).astype(jnp.bfloat16)
    return (high, low)


def split_table(table):
    table = np.asarray(table, np.float32)
    high = table.astype(jnp.bfloat16)
    low = (table - high.astype(np.float32)).astype(jnp.bfloat16)
    return (high, low)


def window_table(cells, samples, columns):
    lane = np.arange(LANES)
    out = np.zeros((cells // samples, LANES, cells), np.float32)
    cell = np.arange(cells)
    per_column = samples // columns
    for line in range(cells // samples):
        out[line] = (lane[:, None] // LOOK_RG == cell[None, :] % per_column) & (
            cell[None, :] // samples == line
        )
    return out.reshape(-1, cells).astype(jnp.bfloat16)


def sample_tables(cells, samples, halves):
    cell = np.arange(cells) % samples
    frequency = np.arange(PATCH)
    forward = []
    place = []
    for half in range(halves):
        position = half * samples + cell
        angle = 2.0 * np.pi * (position[:, None] * frequency[None, :] % PATCH) / PATCH
        forward.append((np.cos(angle), np.sin(angle)))
        place.append(np.arange(halves * samples)[:, None] == position[None, :])
    real = [np.concatenate([c, -s, -s, -c], 1) for c, s in forward]
    imag = [np.concatenate([s, c, c, -s], 1) for c, s in forward]
    return (np.stack(real + imag), np.stack(place).astype(np.float32).astype(jnp.bfloat16))


def line_tables():
    row = np.arange(HALF)
    frequency = np.arange(PATCH)
    angle = 2.0 * np.pi * (frequency[:, None] * row[None, :] % PATCH) / PATCH
    cosine, sine = np.cos(angle), np.sin(angle)
    ramp = 1.0 - np.abs(np.arange(PATCH) + 0.5 - HALF) / HALF
    first, second = ramp[None, :HALF], ramp[None, HALF:]
    flip = (1.0 - 2.0 * (frequency % 2))[:, None]
    none = np.zeros_like(angle)

    def back(wave):
        top = np.concatenate([second * wave, first * wave, none, none], 0)
        bottom = np.concatenate([none, none, second * flip * wave, first * wave], 0)
        return np.concatenate([top, bottom], 1)

    end = np.concatenate([back(cosine), back(sine)], 0) / PATCH**2
    return (np.concatenate([cosine, sine], 1), end)


def back_table(pairs):
    frequency = np.arange(PATCH)
    column = np.arange(HALF)
    angle = 2.0 * np.pi * (column[:, None] * frequency[None, :] % PATCH) / PATCH
    c, s = np.cos(angle), np.sin(angle)
    direct = np.concatenate([np.concatenate([c, -s], 1), np.concatenate([s, c], 1)], 0)
    turned = np.concatenate([np.concatenate([-s, -c], 1), np.concatenate([c, -s], 1)], 0)
    identity = np.eye(pairs)
    return np.concatenate([np.kron(identity, direct), np.kron(identity, turned)], 0)


def dot(left, right):
    return jnp.dot(left, right, preferred_element_type=jnp.float32)


def dot_rows(left, right):
    return lax.dot_general(
        left, right, (((1,), (1,)), ((), ())), preferred_element_type=jnp.float32
    )


def products_kernel(
    place_ref, pair_ref, own_ref, near_ref, far_ref, last_ref, window_ref,
    out0_ref, out1_ref, out2_ref, out3_ref,
    plain_ref, turned_ref, high_ref, low_ref, sum_ref, root_ref, scale_ref,
):
    group = place_ref[0]
    dates_here = own_ref.shape[0]
    dates = plain_ref.shape[0]
    looks = plain_ref.shape[2]
    pair_total = pair_ref.shape[0] // 2
    even = lax.broadcasted_iota(jnp.int32, (looks, 8, LANES), 1) % 2 == 0
    for offset, ref in enumerate((own_ref, near_ref, far_ref, last_ref)):
        base = (group ^ offset) * dates_here
        for index in range(dates_here):
            values = ref[index].astype(jnp.float32).reshape(looks, 2, 8, LANES)
            for part in range(2):
                lines = values[:, part]
                plain_ref[base + index, part] = lines
                turned_ref[base + index, part] = jnp.where(
                    even, -pltpu.roll(lines, 7, 1), pltpu.roll(lines, 1, 1)
                )

    def keep(slot, first, second):
        joined = jnp.concatenate([first, second], axis=1)
        high, low = rounded_parts(joined)
        for look in range(looks):
            columns = slice(look * LANES, (look + 1) * LANES)
            high_ref[slot, :, columns] = high[look]
            low_ref[slot, :, columns] = low[look]

    def one_pair(index, carry):
        earlier = pair_ref[index]
        later = pair_ref[pair_total + index]
        left0 = plain_ref[earlier, 0]
        left1 = plain_ref[earlier, 1]
        real = left0 * plain_ref[later, 0] + left1 * plain_ref[later, 1]
        imag = left0 * turned_ref[later, 0] + left1 * turned_ref[later, 1]
        keep(index, real, imag)
        return carry

    def two_dates(index, carry):
        def power(date):
            return plain_ref[date, 0] * plain_ref[date, 0] + plain_ref[date, 1] * plain_ref[date, 1]

        keep(pair_total + index, power(2 * index), power(2 * index + 1))
        return carry

    lax.fori_loop(0, dates // 2, two_dates, 0)
    lax.fori_loop(0, pair_total, one_pair, 0)
    rows = high_ref.shape[0] * 16
    width = high_ref.shape[2]
    table = window_ref[...]
    sum_ref[...] = dot(high_ref[...].reshape(rows, width), table) + dot(
        low_ref[...].reshape(rows, width), table
    )
    share = 1.0 / (LOOK_AZ * LOOK_RG)

    def fold(start, count):
        def added(picks):
            total = sum_ref[pl.ds(start * 8 + picks[0], count, stride=8), :]
            for pick in picks[1:]:
                total = total + sum_ref[pl.ds(start * 8 + pick, count, stride=8), :]
            return total

        second = lax.broadcasted_iota(jnp.int32, (count, LANES), 1) // 8 % 2 == 1
        return jnp.where(second, added((2, 3, 6, 7)), added((0, 1, 4, 5))) * share

    root_ref[...] = lax.rsqrt(fold(2 * pair_total, dates) + EPSILON)
    for index in range(pair_total):
        earlier = root_ref[pl.ds(pair_ref[index], 1), :]
        later = root_ref[pl.ds(pair_ref[pair_total + index], 1), :]
        scale_ref[2 * index : 2 * index + 2, :] = jnp.broadcast_to(earlier * later, (2, LANES))
    ratio = fold(0, 2 * pair_total) * scale_ref[...]
    each = ratio.shape[0] // 4
    for index, ref in enumerate((out0_ref, out1_ref, out2_ref, out3_ref)):
        ref[...] = ratio[index * each : (index + 1) * each]


def filter_kernel(
    place_ref, z0_ref, z1_ref, z2_ref, z3_ref, q1_ref, q2_ref, q3_ref,
    sample_high_ref, sample_low_ref, place_table_ref, line_high_ref, line_low_ref,
    back_high_ref, back_low_ref, end_high_ref, end_low_ref,
    filtered_ref, coherence_ref, field_ref, size_ref,
):
    here = place_ref[0]
    pairs = coherence_ref.shape[0]
    rows = 2 * pairs
    lane = lax.broadcasted_iota(jnp.int32, (8, LANES), 1)
    line = lax.broadcasted_iota(jnp.int32, (8, LANES), 0)
    inside = lane // 16 == line
    along = (z0_ref, z1_ref, z2_ref, z3_ref)
    across = (None, q1_ref, q2_ref, q3_ref)
    for far in range(4):
        for near in range(4):
            source = here ^ (4 * far + near)
            core = source & 1
            half = (source >> 1) & 1
            block = core * 4 + (source >> 2)
            if near == 0:
                values = along[far][0:rows, :]
            else:
                values = across[near][far * rows : (far + 1) * rows, :]
            for pair in range(pairs):
                real = values[2 * pair : 2 * pair + 1]
                imag = values[2 * pair + 1 : 2 * pair + 2]
                size = jnp.sqrt(real * real + imag * imag)
                target = pl.ds(pl.multiple_of(pair * PATCH + block * 8, 8), 8)
                field_ref[half, target, :] = jnp.where(
                    inside, jnp.broadcast_to(real, (8, LANES)), 0.0
                )
                field_ref[2 + half, target, :] = jnp.where(
                    inside, jnp.broadcast_to(imag, (8, LANES)), 0.0
                )
                size_ref[half, target, :] = jnp.where(
                    inside, jnp.broadcast_to(size, (8, LANES)), 0.0
                )
    for pair in range(pairs):
        lines = slice(pair * PATCH, (pair + 1) * PATCH)
        magnitude = dot_rows(
            place_table_ref[0], size_ref[0, lines].astype(jnp.bfloat16)
        ) + dot_rows(place_table_ref[1], size_ref[1, lines].astype(jnp.bfloat16))
        coherence_ref[pair] = magnitude.astype(coherence_ref.dtype)
    spread = None
    for index in range(4):
        high, low = rounded_parts(field_ref[index])
        table = sample_high_ref[index]
        term = dot(high, table) + dot(low, table) + dot(high, sample_low_ref[index])
        spread = term if spread is None else spread + term
    columns = []
    for half in range(2):
        for pair in range(pairs):
            start = pair * PATCH + half * HALF
            part = spread[start : start + HALF]
            columns.append(jnp.concatenate([part[:, :LANES], part[:, LANES:]], 0))
    high, low = rounded_parts(jnp.concatenate(columns, 1))
    spectrum = (
        dot(line_high_ref[...], high) + dot(line_high_ref[...], low) + dot(line_low_ref[...], high)
    )
    width = pairs * LANES
    top = spectrum[:, :width]
    bottom = spectrum[:, width:]
    sign = 1.0 - 2.0 * (lax.broadcasted_iota(jnp.int32, (PATCH, width), 0) % 2).astype(jnp.float32)
    weighted = []
    for patch in (top, top + sign * bottom, bottom):
        parts = []
        for pair in range(pairs):
            values = patch[:, pair * LANES : (pair + 1) * LANES]
            square = values * values
            energy = square + pltpu.roll(square, LANES // 2, 1)
            weight = lax.rsqrt(lax.rsqrt(energy + 1.0))
            total = jnp.sum(weight, axis=(0, 1), keepdims=True)
            parts.append(values * weight * ((2.0 * PATCH * PATCH) / total))
        weighted.append(jnp.concatenate(parts, 1))
    weighted = [weighted[0], weighted[1], weighted[1], weighted[2]]
    high, low = rounded_parts(jnp.concatenate(weighted, 0))
    back = (
        dot_rows(back_high_ref[...], high)
        + dot_rows(back_high_ref[...], low)
        + dot_rows(back_low_ref[...], high)
    )
    high, low = rounded_parts(jnp.concatenate([back[: width // 2], back[width // 2 :]], 1))
    lines = dot(high, end_high_ref[...]) + dot(low, end_high_ref[...]) + dot(high, end_low_ref[...])
    filtered_ref[...] = lines.reshape(filtered_ref.shape).astype(filtered_ref.dtype)


def fast_local(acquisitions, date_pairs, sizes):
    depth, across, cores = sizes
    total = depth * across * cores
    dates_here, line_count, _, sample_count = acquisitions.shape
    columns = sample_count // LANES
    lines_each = line_count // depth
    rows = lines_each * columns * 2
    look_lines = lines_each // LOOK_AZ
    look_samples = sample_count // LOOK_RG
    cells = look_lines * look_samples
    pairs_here = date_pairs.shape[1]
    pair_total = pairs_here * total
    dates = dates_here * depth
    group = lax.axis_index("date")
    here = lax.axis_index(("date", "rng", "az"))
    names = ("date", "rng", "az")

    def swap(values, offset):
        return lax.ppermute(values, names, [(i, i ^ offset) for i in range(total)])

    view = acquisitions.reshape(dates_here, line_count, 2, columns, LANES)
    view = view.transpose(0, 1, 3, 2, 4).reshape(dates_here, line_count * columns * 2, LANES)

    def block(index):
        return lax.dynamic_slice_in_dim(view, index * rows, rows, 1)

    step = across * cores
    received = {3: swap(block(group ^ 3), 3 * step)}
    listed = date_pairs.T[None]
    listed = jnp.concatenate([listed, swap(listed, 1)], 0)
    late, listed = lax.optimization_barrier((group, listed))
    received[2] = swap(block(late ^ 2), 2 * step)
    received[1] = swap(block(late ^ 1), step)
    own = block(late)
    offset = 2
    while offset < total:
        listed = jnp.concatenate([listed, swap(listed, offset)], 0)
        offset *= 2
    pair_list = listed.reshape(pair_total, 2).T.reshape(-1)
    width = look_lines * LANES
    slots = pair_total + dates // 2
    vmem = pl.BlockSpec(memory_space=pltpu.VMEM)
    smem = pl.BlockSpec(memory_space=pltpu.SMEM)
    piece = jax.ShapeDtypeStruct((2 * pair_total // depth, cells), jnp.float32)
    pieces = pl.pallas_call(
        products_kernel,
        name="products",
        out_shape=[piece] * depth,
        in_specs=[smem, smem] + [vmem] * 5,
        out_specs=[vmem] * depth,
        scratch_shapes=[
            pltpu.VMEM((dates, 2, look_lines, 8, LANES), jnp.float32),
            pltpu.VMEM((dates, 2, look_lines, 8, LANES), jnp.float32),
            pltpu.VMEM((slots, 16, width), jnp.bfloat16),
            pltpu.VMEM((slots, 16, width), jnp.bfloat16),
            pltpu.VMEM((slots * 16, cells), jnp.float32),
            pltpu.VMEM((dates, cells), jnp.float32),
            pltpu.VMEM((2 * pair_total, cells), jnp.float32),
        ],
        compiler_params=pltpu.CompilerParams(vmem_limit_bytes=12 << 20),
    )(
        group.reshape(1),
        pair_list,
        own,
        received[1],
        received[2],
        received[3],
        jnp.asarray(window_table(cells, look_samples, columns)),
    )
    arrived = [pieces[0]] + [None] * (depth - 1)
    for k in (3, 2, 1):
        arrived[k] = swap(pieces[k], k * step)
    each = 2 * pairs_here
    sideways = []
    for k in (3, 2, 1):
        payload = jnp.concatenate([a[k * each : (k + 1) * each] for a in arrived], 0)
        sideways.append(swap(payload, k))
    sideways = sideways[::-1]
    sample_table, place_table = sample_tables(cells, look_samples, across)
    line_table, end_table = line_tables()
    tables = []
    for table in (sample_table, None, line_table, back_table(pairs_here), end_table):
        tables += [place_table] if table is None else list(split_table(table))
    filtered, coherence = pl.pallas_call(
        filter_kernel,
        name="filter",
        out_shape=[
            jax.ShapeDtypeStruct((pairs_here, 2, HALF, PATCH), jnp.bfloat16),
            jax.ShapeDtypeStruct((pairs_here, HALF, PATCH), jnp.bfloat16),
        ],
        in_specs=[smem] + [vmem] * (depth + 3 + len(tables)),
        out_specs=[vmem, vmem],
        scratch_shapes=[
            pltpu.VMEM((4, pairs_here * PATCH, cells), jnp.float32),
            pltpu.VMEM((2, pairs_here * PATCH, cells), jnp.float32),
        ],
        compiler_params=pltpu.CompilerParams(vmem_limit_bytes=8 << 20),
    )(here.reshape(1), *arrived, *sideways, *[jnp.asarray(t) for t in tables])
    return (filtered.transpose(0, 1, 3, 2), coherence.transpose(0, 2, 1))


def fits(acquisitions, date_pairs, sizes):
    depth, across, cores = sizes
    _, line_count, _, sample_count = acquisitions.shape
    look_lines = line_count // depth // LOOK_AZ
    look_samples = sample_count // LOOK_RG
    return (
        sizes == (4, 2, 2)
        and line_count % (depth * LOOK_AZ) == 0
        and sample_count == 2 * LANES
        and look_lines == 8
        and look_lines * look_samples == LANES
        and line_count * cores == LOOK_AZ * PATCH
        and sample_count * across == LOOK_RG * HALF
        and date_pairs.shape[1] == 2
    )


def solution(mesh):
    sizes = tuple(mesh.shape[name] for name in ("date", "rng", "az"))

    def chosen(acquisitions, date_pairs):
        if fits(acquisitions, date_pairs, sizes):
            return fast_local(acquisitions, date_pairs, sizes)
        return local(acquisitions, date_pairs)

    return jax.shard_map(
        chosen,
        mesh=mesh,
        in_specs=(P(("tile", "date"), "az", None, "rng"), P(None, ("date", "rng", "az"))),
        out_specs=(
            P(("tile", "date", "rng", "az"), None, None, None),
            P(("tile", "date", "rng", "az"), None, None),
        ),
        check_vma=False,
    )
```

profile of v0, /device:TPU:0, one launch (start us, length us, event | category | flops | bytes accessed | tf_op | source)
XLA Modules:
  0.0 41.2 jit_solution(1415487752600389783)
XLA Ops:
  0.6 0.0 copy-start.10
  0.6 0.7 %copy-done.10 = s32[2,2]{1,0:T(2,128)S(1)} copy-done((s32[2,2]{1,0:T(2,128)S(1)}, s32[2,2]{1,0:T(2,128)}, u32[]{:S(2)}) %copy-start.10) | copy-done | bytes 40
  1.3 0.1 copy.29
  1.4 0.5 %collective-permute-start = (s32[1,2,2]{2,1,0:T(2,128)S(1)}, s32[1,2,2]{2,1,0:T(2,128)S(1)}, u32[]{:S(2)}, u32[]{:S(2)}) collective-permute-start(s32[1,2,2]{2,1,0:T(2,128)S(1)} %bitcast.15), channel_id=1, source_target_pairs={{0,1},{1,0},{2,3},{3,2},{4,5},{5,4},{6,7},{7,6},{8,9},{9,8},{10,11... | collective-permute-start | bytes 56 | tf_op jit(solution)/shard_map/ppermute | solution.py:444
  1.9 0.8 %collective-permute-done = s32[1,2,2]{2,1,0:T(2,128)S(1)} collective-permute-done((s32[1,2,2]{2,1,0:T(2,128)S(1)}, s32[1,2,2]{2,1,0:T(2,128)S(1)}, u32[]{:S(2)}, u32[]{:S(2)}) %collective-permute-start) | collective-permute-done | bytes 48 | tf_op jit(solution)/shard_map/ppermute | solution.py:444
  2.7 0.1 copy.33
  2.8 2.8 %collective-permute-start.1 = (s32[2,2,2]{2,1,0:T(2,128)S(1)}, s32[2,2,2]{2,1,0:T(2,128)S(1)}, u32[]{:S(2)}, u32[]{:S(2)}) collective-permute-start(s32[2,2,2]{2,1,0:T(2,128)S(1)} %pad_add_fusion.1), channel_id=1, source_target_pairs={{0,2},{1,3},{2,0},{3,1},{4,6},{5,7},{6,4},{7,5},{8,10},{9,11},{10,... | collective-permute-start | bytes 104 | tf_op jit(solution)/shard_map/ppermute | solution.py:444
  5.6 0.0 copy-start
  5.6 0.0 copy-start.6
  5.6 1.2 %constant_dynamic-slice_fusion = (bf16[4,128,128]{2,1,0:T(8,128)(2,1)S(1)}, bf16[4,128,128]{2,1,0:T(8,128)(2,1)S(1)}, bf16[4,128,128]{2,1,0:T(8,128)(2,1)S(1)}, bf16[4,128,128]{2,1,0:T(8,128)(2,1)S(1)}) fusion(bf16[4,512,128]{2,1,0:T(8,128)(2,1)} %bitcast.14, s32[]{:T(128)S(6)} %select_n.15, s32[]{:T(128)S(6)} %select_n.14, s32[]{:T(128)S(6)} %select_n.13, ...), kind=kLoop, calls=%fused_computation.7 | loop fusion | bytes 1048592 | tf_op jit(solution)/shard_map/dynamic_slice | solution.py:450
  6.8 3.7 %collective-permute-start.6 = (bf16[4,128,128]{2,1,0:T(8,128)(2,1)S(1)}, bf16[4,128,128]{2,1,0:T(8,128)(2,1)S(1)}, u32[]{:S(2)}, u32[]{:S(2)}) collective-permute-start(bf16[4,128,128]{2,1,0:T(8,128)(2,1)S(1)} %get-tuple-element.18), channel_id=1, source_target_pairs={{0,12},{1,13},{2,14},{3,15},{4,8},{5,9},{6,10},{7,11},{8,4},{9,5},... | collective-permute-start | bytes 393224 | tf_op jit(solution)/shard_map/ppermute | solution.py:444
  10.5 0.0 collective-permute-start.5
  10.5 0.8 %collective-permute-start.4 = (bf16[4,128,128]{2,1,0:T(8,128)(2,1)S(1)}, bf16[4,128,128]{2,1,0:T(8,128)(2,1)S(1)}, u32[]{:S(2)}, u32[]{:S(2)}) collective-permute-start(bf16[4,128,128]{2,1,0:T(8,128)(2,1)S(1)} %get-tuple-element.20), channel_id=1, source_target_pairs={{0,4},{1,5},{2,6},{3,7},{4,0},{5,1},{6,2},{7,3},{8,12},{9,13},{10,... | collective-permute-start | bytes 393224 | tf_op jit(solution)/shard_map/ppermute | solution.py:444
  11.3 0.0 collective-permute-done.1
  11.3 1.3 %collective-permute-start.2 = (s32[4,2,2]{2,1,0:T(2,128)S(1)}, s32[4,2,2]{2,1,0:T(2,128)S(1)}, u32[]{:S(2)}, u32[]{:S(2)}) collective-permute-start(s32[4,2,2]{2,1,0:T(2,128)S(1)} %pad_add_fusion), channel_id=1, source_target_pairs={{0,4},{1,5},{2,6},{3,7},{4,0},{5,1},{6,2},{7,3},{8,12},{9,13},{10,... | collective-permute-start | bytes 200 | tf_op jit(solution)/shard_map/ppermute | solution.py:444
  12.6 0.1 copy.34
  12.7 6.4 %collective-permute-done.2 = s32[4,2,2]{2,1,0:T(2,128)S(1)} collective-permute-done((s32[4,2,2]{2,1,0:T(2,128)S(1)}, s32[4,2,2]{2,1,0:T(2,128)S(1)}, u32[]{:S(2)}, u32[]{:S(2)}) %collective-permute-start.2) | collective-permute-done | bytes 96 | tf_op jit(solution)/shard_map/ppermute | solution.py:444
  19.1 0.1 copy.35
  19.2 0.1 pad_add_fusion.2
  19.2 1.3 %collective-permute-start.3 = (s32[8,2,2]{0,2,1:T(2,128)S(1)}, s32[8,2,2]{0,2,1:T(2,128)S(1)}, u32[]{:S(2)}, u32[]{:S(2)}) collective-permute-start(s32[8,2,2]{0,2,1:T(2,128)S(1)} %pad_add_fusion.2), channel_id=1, source_target_pairs={{0,8},{1,9},{2,10},{3,11},{4,12},{5,13},{6,14},{7,15},{8,0},{9,1},... | collective-permute-start | bytes 392 | tf_op jit(solution)/shard_map/ppermute | solution.py:444
  20.5 3.2 %collective-permute-done.3 = s32[8,2,2]{0,2,1:T(2,128)S(1)} collective-permute-done((s32[8,2,2]{0,2,1:T(2,128)S(1)}, s32[8,2,2]{0,2,1:T(2,128)S(1)}, u32[]{:S(2)}, u32[]{:S(2)}) %collective-permute-start.3) | collective-permute-done | bytes 160 | tf_op jit(solution)/shard_map/ppermute | solution.py:444
  23.7 0.0 copy-start.9
  23.7 0.1 pad_add_fusion.3
  23.8 0.1 copy.36
  23.9 0.0 copy-start.8
  23.9 0.1 reshape.24
  24.0 0.1 reshape.25.pair_ref
  24.1 0.0 collective-permute-done.6.last_ref
  24.1 0.0 collective-permute-done.5.far_ref
  24.1 0.0 collective-permute-done.4.near_ref
  24.1 0.0 copy-done
  24.1 0.0 copy-start.1
  24.1 0.0 copy-start.2
  24.1 0.0 copy-start.4
  24.1 0.0 copy-start.5
  24.2 2.7 %products.1 = (f32[16,128]{1,0:T(8,128)S(1)}, f32[16,128]{1,0:T(8,128)S(1)}, f32[16,128]{1,0:T(8,128)S(1)}, f32[16,128]{1,0:T(8,128)S(1)}) custom-call(s32[1]{0:T(128)} %bitcast.1.place_ref, s32[64]{0:T(128)S(1)} %reshape.25.pair_ref, bf16[4,128,128]{2,1,0:T(8,128)(2,1)S(1)} %get-tuple-element.21.own_ref, ...), custom_call_target="tpu_custom_call" | custom-call | tf_op jit(solution)/shard_map/products/pallas_call | solution.py:470
  26.8 0.0 copy-start.3
  26.9 2.5 %collective-permute-start.7 = (f32[16,128]{1,0:T(8,128)S(1)}, f32[16,128]{1,0:T(8,128)S(1)}, u32[]{:S(2)}, u32[]{:S(2)}) collective-permute-start(f32[16,128]{1,0:T(8,128)S(1)} %get-tuple-element.13), channel_id=1, source_target_pairs={{0,4},{1,5},{2,6},{3,7},{4,0},{5,1},{6,2},{7,3},{8,12},{9,13},{10,... | collective-permute-start | bytes 24584 | tf_op jit(solution)/shard_map/ppermute | solution.py:444
  29.4 0.0 collective-permute-start.8
  29.4 2.4 %collective-permute-start.9 = (f32[16,128]{1,0:T(8,128)S(1)}, f32[16,128]{1,0:T(8,128)S(1)}, u32[]{:S(2)}, u32[]{:S(2)}) collective-permute-start(f32[16,128]{1,0:T(8,128)S(1)} %get-tuple-element.15), channel_id=1, source_target_pairs={{0,12},{1,13},{2,14},{3,15},{4,8},{5,9},{6,10},{7,11},{8,4},{9,5},... | collective-permute-start | bytes 24584 | tf_op jit(solution)/shard_map/ppermute | solution.py:444
  31.9 0.0 collective-permute-done.7.z1_ref
  31.9 2.1 %collective-permute-done.8.z2_ref = f32[16,128]{1,0:T(8,128)S(1)} collective-permute-done((f32[16,128]{1,0:T(8,128)S(1)}, f32[16,128]{1,0:T(8,128)S(1)}, u32[]{:S(2)}, u32[]{:S(2)}) %collective-permute-start.8) | collective-permute-done | bytes 8224 | tf_op jit(solution)/shard_map/ppermute | solution.py:444
  34.0 0.9 %collective-permute-done.9.z3_ref = f32[16,128]{1,0:T(8,128)S(1)} collective-permute-done((f32[16,128]{1,0:T(8,128)S(1)}, f32[16,128]{1,0:T(8,128)S(1)}, u32[]{:S(2)}, u32[]{:S(2)}) %collective-permute-start.9) | collective-permute-done | bytes 8224 | tf_op jit(solution)/shard_map/ppermute | solution.py:444
  34.9 0.1 collective-permute-start.10
  35.0 0.6 %collective-permute-start.11 = (f32[16,128]{1,0:T(8,128)S(1)}, f32[16,128]{1,0:T(8,128)S(1)}, u32[]{:S(2)}, u32[]{:S(2)}) collective-permute-start(f32[16,128]{1,0:T(8,128)S(1)} %pad_maximum_fusion.1), channel_id=1, source_target_pairs={{0,2},{1,3},{2,0},{3,1},{4,6},{5,7},{6,4},{7,5},{8,10},{9,11},{10,... | collective-permute-start | bytes 24584 | tf_op jit(solution)/shard_map/ppermute | solution.py:444
  35.6 0.0 copy-start.7
  35.6 1.4 %collective-permute-start.12 = (f32[16,128]{1,0:T(8,128)S(1)}, f32[16,128]{1,0:T(8,128)S(1)}, u32[]{:S(2)}, u32[]{:S(2)}) collective-permute-start(f32[16,128]{1,0:T(8,128)S(1)} %pad_maximum_fusion.2), channel_id=1, source_target_pairs={{0,3},{1,2},{2,1},{3,0},{4,7},{5,6},{6,5},{7,4},{8,11},{9,10},{10,... | collective-permute-start | bytes 24584 | tf_op jit(solution)/shard_map/ppermute | solution.py:444
  37.0 0.0 collective-permute-done.10.q1_ref
  37.0 1.8 %collective-permute-done.11.q2_ref = f32[16,128]{1,0:T(8,128)S(1)} collective-permute-done((f32[16,128]{1,0:T(8,128)S(1)}, f32[16,128]{1,0:T(8,128)S(1)}, u32[]{:S(2)}, u32[]{:S(2)}) %collective-permute-start.11) | collective-permute-done | bytes 8224 | tf_op jit(solution)/shard_map/ppermute | solution.py:444
  38.7 0.0 collective-permute-done.12.q3_ref
  38.8 0.0 copy-done.6
  38.8 0.0 copy-done.9
  38.8 0.0 copy-done.8
  38.8 0.0 copy-done.1
  38.8 0.0 copy-done.2
  38.8 0.0 copy-done.4
  38.8 0.0 copy-done.5
  38.8 0.0 copy-done.3
  38.8 0.0 copy-done.7
  38.9 2.3 %filter.1 = (bf16[2,2,32,64]{3,2,1,0:T(8,128)(2,1)}, bf16[2,32,64]{2,1,0:T(8,128)(2,1)}) custom-call(s32[1]{0:T(128)} %bitcast.place_ref, f32[16,128]{1,0:T(8,128)S(1)} %get-tuple-element.12.z0_ref, f32[16,128]{1,0:T(8,128)S(1)} %collective-permute-done.7.z1_ref, f32[16,128]{1,0:T(8,128)S(1)} %collective-permute-done.8.z2_ref, ...), custom_call_target="tpu_custom_call" | custom-call | tf_op jit(solution)/shard_map/filter/pallas_call | solution.py:509
  (9 shorter events, 0.1 us)
Async XLA Ops:
  0.6 0.7 %copy-start.10 = (s32[2,2]{1,0:T(2,128)S(1)}, s32[2,2]{1,0:T(2,128)}, u32[]{:S(2)}) copy-start(s32[2,2]{1,0:T(2,128)} %param.13) | copy-start | bytes 52
  1.4 1.3 %collective-permute-start = (s32[1,2,2]{2,1,0:T(2,128)S(1)}, s32[1,2,2]{2,1,0:T(2,128)S(1)}, u32[]{:S(2)}, u32[]{:S(2)}) collective-permute-start(s32[1,2,2]{2,1,0:T(2,128)S(1)} %bitcast.15), channel_id=1, source_target_pairs={{0,1},{1,0},{2,3},{3,2},{4,5},{5,4},{6,7},{7,6},{8,9},{9,8},{10,11... | collective-permute-start | bytes 56 | tf_op jit(solution)/shard_map/ppermute | solution.py:444
  2.8 8.5 %collective-permute-start.1 = (s32[2,2,2]{2,1,0:T(2,128)S(1)}, s32[2,2,2]{2,1,0:T(2,128)S(1)}, u32[]{:S(2)}, u32[]{:S(2)}) collective-permute-start(s32[2,2,2]{2,1,0:T(2,128)S(1)} %pad_add_fusion.1), channel_id=1, source_target_pairs={{0,2},{1,3},{2,0},{3,1},{4,6},{5,7},{6,4},{7,5},{8,10},{9,11},{10,... | collective-permute-start | bytes 104 | tf_op jit(solution)/shard_map/ppermute | solution.py:444
  5.6 18.5 %copy-start = (bf16[1024,128]{1,0:T(8,128)(2,1)S(1)}, bf16[1024,128]{1,0:T(8,128)(2,1)}, u32[]{:S(2)}) copy-start(bf16[1024,128]{1,0:T(8,128)(2,1)} %constant.45.clone.window_ref) | copy-start | bytes 786436
  5.6 33.1 %copy-start.6 = (bf16[256,256]{1,0:T(8,128)(2,1)S(1)}, bf16[256,256]{1,0:T(8,128)(2,1)}, u32[]{:S(2)}) copy-start(bf16[256,256]{1,0:T(8,128)(2,1)} %constant.51.clone.back_high_ref) | copy-start | bytes 393220
  6.8 17.2 %collective-permute-start.6 = (bf16[4,128,128]{2,1,0:T(8,128)(2,1)S(1)}, bf16[4,128,128]{2,1,0:T(8,128)(2,1)S(1)}, u32[]{:S(2)}, u32[]{:S(2)}) collective-permute-start(bf16[4,128,128]{2,1,0:T(8,128)(2,1)S(1)} %get-tuple-element.18), channel_id=1, source_target_pairs={{0,12},{1,13},{2,14},{3,15},{4,8},{5,9},{6,10},{7,11},{8,4},{9,5},... | collective-permute-start | bytes 393224 | tf_op jit(solution)/shard_map/ppermute | solution.py:444
  10.5 13.6 %collective-permute-start.5 = (bf16[4,128,128]{2,1,0:T(8,128)(2,1)S(1)}, bf16[4,128,128]{2,1,0:T(8,128)(2,1)S(1)}, u32[]{:S(2)}, u32[]{:S(2)}) collective-permute-start(bf16[4,128,128]{2,1,0:T(8,128)(2,1)S(1)} %get-tuple-element.19), channel_id=1, source_target_pairs={{0,8},{1,9},{2,10},{3,11},{4,12},{5,13},{6,14},{7,15},{8,0},{9,1},... | collective-permute-start | bytes 393224 | tf_op jit(solution)/shard_map/ppermute | solution.py:444
  10.5 13.6 %collective-permute-start.4 = (bf16[4,128,128]{2,1,0:T(8,128)(2,1)S(1)}, bf16[4,128,128]{2,1,0:T(8,128)(2,1)S(1)}, u32[]{:S(2)}, u32[]{:S(2)}) collective-permute-start(bf16[4,128,128]{2,1,0:T(8,128)(2,1)S(1)} %get-tuple-element.20), channel_id=1, source_target_pairs={{0,4},{1,5},{2,6},{3,7},{4,0},{5,1},{6,2},{7,3},{8,12},{9,13},{10,... | collective-permute-start | bytes 393224 | tf_op jit(solution)/shard_map/ppermute | solution.py:444
  11.3 7.8 %collective-permute-start.2 = (s32[4,2,2]{2,1,0:T(2,128)S(1)}, s32[4,2,2]{2,1,0:T(2,128)S(1)}, u32[]{:S(2)}, u32[]{:S(2)}) collective-permute-start(s32[4,2,2]{2,1,0:T(2,128)S(1)} %pad_add_fusion), channel_id=1, source_target_pairs={{0,4},{1,5},{2,6},{3,7},{4,0},{5,1},{6,2},{7,3},{8,12},{9,13},{10,... | collective-permute-start | bytes 200 | tf_op jit(solution)/shard_map/ppermute | solution.py:444
  19.2 4.5 %collective-permute-start.3 = (s32[8,2,2]{0,2,1:T(2,128)S(1)}, s32[8,2,2]{0,2,1:T(2,128)S(1)}, u32[]{:S(2)}, u32[]{:S(2)}) collective-permute-start(s32[8,2,2]{0,2,1:T(2,128)S(1)} %pad_add_fusion.2), channel_id=1, source_target_pairs={{0,8},{1,9},{2,10},{3,11},{4,12},{5,13},{6,14},{7,15},{8,0},{9,1},... | collective-permute-start | bytes 392 | tf_op jit(solution)/shard_map/ppermute | solution.py:444
  23.7 15.1 %copy-start.9 = (bf16[2,32,128]{2,1,0:T(8,128)(2,1)S(1)}, bf16[2,32,128]{2,1,0:T(8,128)(2,1)}, u32[]{:S(2)}) copy-start(bf16[2,32,128]{2,1,0:T(8,128)(2,1)} %constant.48.clone.place_table_ref) | copy-start | bytes 49156
  23.9 14.9 %copy-start.8 = (bf16[64,64]{1,0:T(8,128)(2,1)S(1)}, bf16[64,64]{1,0:T(8,128)(2,1)}, u32[]{:S(2)}) copy-start(bf16[64,64]{1,0:T(8,128)(2,1)} %constant.49.clone.line_high_ref) | copy-start | bytes 24580
  24.1 14.7 %copy-start.1 = (bf16[4,128,256]{2,1,0:T(8,128)(2,1)S(1)}, bf16[4,128,256]{2,1,0:T(8,128)(2,1)}, u32[]{:S(2)}) copy-start(bf16[4,128,256]{2,1,0:T(8,128)(2,1)} %constant.47.clone.sample_low_ref) | copy-start | bytes 786436
  24.1 14.7 %copy-start.2 = (bf16[4,128,256]{2,1,0:T(8,128)(2,1)S(1)}, bf16[4,128,256]{2,1,0:T(8,128)(2,1)}, u32[]{:S(2)}) copy-start(bf16[4,128,256]{2,1,0:T(8,128)(2,1)} %constant.46.clone.sample_high_ref) | copy-start | bytes 786436
  24.1 14.7 %copy-start.4 = (bf16[512,64]{1,0:T(8,128)(2,1)S(1)}, bf16[512,64]{1,0:T(8,128)(2,1)}, u32[]{:S(2)}) copy-start(bf16[512,64]{1,0:T(8,128)(2,1)} %constant.53.clone.end_high_ref) | copy-start | bytes 196612
  24.1 14.7 %copy-start.5 = (bf16[256,256]{1,0:T(8,128)(2,1)S(1)}, bf16[256,256]{1,0:T(8,128)(2,1)}, u32[]{:S(2)}) copy-start(bf16[256,256]{1,0:T(8,128)(2,1)} %constant.52.clone.back_low_ref) | copy-start | bytes 393220
  26.8 12.0 %copy-start.3 = (bf16[512,64]{1,0:T(8,128)(2,1)S(1)}, bf16[512,64]{1,0:T(8,128)(2,1)}, u32[]{:S(2)}) copy-start(bf16[512,64]{1,0:T(8,128)(2,1)} %constant.54.clone.end_low_ref) | copy-start | bytes 196612
  26.9 5.0 %collective-permute-start.7 = (f32[16,128]{1,0:T(8,128)S(1)}, f32[16,128]{1,0:T(8,128)S(1)}, u32[]{:S(2)}, u32[]{:S(2)}) collective-permute-start(f32[16,128]{1,0:T(8,128)S(1)} %get-tuple-element.13), channel_id=1, source_target_pairs={{0,4},{1,5},{2,6},{3,7},{4,0},{5,1},{6,2},{7,3},{8,12},{9,13},{10,... | collective-permute-start | bytes 24584 | tf_op jit(solution)/shard_map/ppermute | solution.py:444
  29.4 4.5 %collective-permute-start.8 = (f32[16,128]{1,0:T(8,128)S(1)}, f32[16,128]{1,0:T(8,128)S(1)}, u32[]{:S(2)}, u32[]{:S(2)}) collective-permute-start(f32[16,128]{1,0:T(8,128)S(1)} %get-tuple-element.14), channel_id=1, source_target_pairs={{0,8},{1,9},{2,10},{3,11},{4,12},{5,13},{6,14},{7,15},{8,0},{9,1},... | collective-permute-start | bytes 24584 | tf_op jit(solution)/shard_map/ppermute | solution.py:444
  29.4 5.4 %collective-permute-start.9 = (f32[16,128]{1,0:T(8,128)S(1)}, f32[16,128]{1,0:T(8,128)S(1)}, u32[]{:S(2)}, u32[]{:S(2)}) collective-permute-start(f32[16,128]{1,0:T(8,128)S(1)} %get-tuple-element.15), channel_id=1, source_target_pairs={{0,12},{1,13},{2,14},{3,15},{4,8},{5,9},{6,10},{7,11},{8,4},{9,5},... | collective-permute-start | bytes 24584 | tf_op jit(solution)/shard_map/ppermute | solution.py:444
  34.9 2.1 %collective-permute-start.10 = (f32[16,128]{1,0:T(8,128)S(1)}, f32[16,128]{1,0:T(8,128)S(1)}, u32[]{:S(2)}, u32[]{:S(2)}) collective-permute-start(f32[16,128]{1,0:T(8,128)S(1)} %pad_maximum_fusion), channel_id=1, source_target_pairs={{0,1},{1,0},{2,3},{3,2},{4,5},{5,4},{6,7},{7,6},{8,9},{9,8},{10,11... | collective-permute-start | bytes 24584 | tf_op jit(solution)/shard_map/ppermute | solution.py:444
  35.0 3.8 %collective-permute-start.11 = (f32[16,128]{1,0:T(8,128)S(1)}, f32[16,128]{1,0:T(8,128)S(1)}, u32[]{:S(2)}, u32[]{:S(2)}) collective-permute-start(f32[16,128]{1,0:T(8,128)S(1)} %pad_maximum_fusion.1), channel_id=1, source_target_pairs={{0,2},{1,3},{2,0},{3,1},{4,6},{5,7},{6,4},{7,5},{8,10},{9,11},{10,... | collective-permute-start | bytes 24584 | tf_op jit(solution)/shard_map/ppermute | solution.py:444
  35.6 3.3 %copy-start.7 = (bf16[64,64]{1,0:T(8,128)(2,1)S(1)}, bf16[64,64]{1,0:T(8,128)(2,1)}, u32[]{:S(2)}) copy-start(bf16[64,64]{1,0:T(8,128)(2,1)} %constant.50.clone.line_low_ref) | copy-start | bytes 24580
  35.6 3.2 %collective-permute-start.12 = (f32[16,128]{1,0:T(8,128)S(1)}, f32[16,128]{1,0:T(8,128)S(1)}, u32[]{:S(2)}, u32[]{:S(2)}) collective-permute-start(f32[16,128]{1,0:T(8,128)S(1)} %pad_maximum_fusion.2), channel_id=1, source_target_pairs={{0,3},{1,2},{2,1},{3,0},{4,7},{5,6},{6,5},{7,4},{8,11},{9,10},{10,... | collective-permute-start | bytes 24584 | tf_op jit(solution)/shard_map/ppermute | solution.py:444
where the time goes:
time: 41.3 us; the launch traced here: 41.2 us
  starting transfers between devices  17.4 us (42%)
  waiting for transfers between devices  15.2 us (37%)
  Pallas kernels  5.02 us (12%)
  local copies, waits for them, and re-layouts  2.57 us (6%)
  between operations  0.79 us (2%)
    ppermute x13, starting transfers between devices, swap(): return lax.ppermute(values, names, [(i, i ^ offset) for i in range(total)])  17.4 us
    ppermute x13, waiting for transfers between devices, swap(): return lax.ppermute(values, names, [(i, i ^ offset) for i in range(total)])  15.2 us
    pallas_call x1, Pallas kernels, fast_local(): pl.pallas_call(products_kernel, name='products', out_shape=[piece] * dept...  2.69 us
    pallas_call x1, Pallas kernels, fast_local(): pl.pallas_call(filter_kernel, name='filter', out_shape=[jax.ShapeDtypeStr...  2.33 us
    dynamic_slice x1, local copies, waits for them, and re-layouts, block(): return lax.dynamic_slice_in_dim(view, index * rows, rows, 1)  1.18 us
  transfers between devices with their start and end apart: 13, of which 6 were waited for; matrix products, arithmetic and copies ran while one was open for 4% of the time, Pallas kernels for 0%

commit v1 on v0

--- a/solution.py
+++ b/solution.py
@@ -260,14 +260,16 @@
 
 def products_kernel(
     place_ref, pair_ref, own_ref, near_ref, far_ref, last_ref, window_ref,
-    out0_ref, out1_ref, out2_ref, out3_ref,
+    out_ref,
     plain_ref, turned_ref, high_ref, low_ref, sum_ref, root_ref, scale_ref,
 ):
     group = place_ref[0]
     dates_here = own_ref.shape[0]
     dates = plain_ref.shape[0]
     looks = plain_ref.shape[2]
-    pair_total = pair_ref.shape[0] // 2
+    owners = pair_ref.shape[0]
+    pairs_here = pair_ref.shape[1] // 2
+    pair_total = owners * pairs_here
     even = lax.broadcasted_iota(jnp.int32, (looks, 8, LANES), 1) % 2 == 0
     for offset, ref in enumerate((own_ref, near_ref, far_ref, last_ref)):
         base = (group ^ offset) * dates_here
@@ -289,8 +291,9 @@
             low_ref[slot, :, columns] = low[look]
 
     def one_pair(index, carry):
-        earlier = pair_ref[index]
-        later = pair_ref[pair_total + index]
+        owner = index // pairs_here
+        earlier = pair_ref[owner, index % pairs_here]
+        later = pair_ref[owner, pairs_here + index % pairs_here]
         left0 = plain_ref[earlier, 0]
         left1 = plain_ref[earlier, 1]
         real = left0 * plain_ref[later, 0] + left1 * plain_ref[later, 1]
@@ -326,53 +329,42 @@
         return jnp.where(second, added((2, 3, 6, 7)), added((0, 1, 4, 5))) * share
 
     root_ref[...] = lax.rsqrt(fold(2 * pair_total, dates) + EPSILON)
-    for index in range(pair_total):
-        earlier = root_ref[pl.ds(pair_ref[index], 1), :]
-        later = root_ref[pl.ds(pair_ref[pair_total + index], 1), :]
-        scale_ref[2 * index : 2 * index + 2, :] = jnp.broadcast_to(earlier * later, (2, LANES))
+    for owner in range(owners):
+        for index in range(pairs_here):
+            earlier = root_ref[pl.ds(pair_ref[owner, index], 1), :]
+            later = root_ref[pl.ds(pair_ref[owner, pairs_here + index], 1), :]
+            start = 2 * (owner * pairs_here + index)
+            scale_ref[start : start + 2, :] = jnp.broadcast_to(earlier * later, (2, LANES))
     ratio = fold(0, 2 * pair_total) * scale_ref[...]
-    each = ratio.shape[0] // 4
-    for index, ref in enumerate((out0_ref, out1_ref, out2_ref, out3_ref)):
-        ref[...] = ratio[index * each : (index + 1) * each]
+    out_ref[...] = ratio.reshape(out_ref.shape)
 
 
 def filter_kernel(
-    place_ref, z0_ref, z1_ref, z2_ref, z3_ref, q1_ref, q2_ref, q3_ref,
-    sample_high_ref, sample_low_ref, place_table_ref, line_high_ref, line_low_ref,
+    ratio_ref, sample_high_ref, sample_low_ref, place_table_ref, line_high_ref, line_low_ref,
     back_high_ref, back_low_ref, end_high_ref, end_low_ref,
     filtered_ref, coherence_ref, field_ref, size_ref,
 ):
-    here = place_ref[0]
     pairs = coherence_ref.shape[0]
-    rows = 2 * pairs
     lane = lax.broadcasted_iota(jnp.int32, (8, LANES), 1)
     line = lax.broadcasted_iota(jnp.int32, (8, LANES), 0)
     inside = lane // 16 == line
-    along = (z0_ref, z1_ref, z2_ref, z3_ref)
-    across = (None, q1_ref, q2_ref, q3_ref)
-    for far in range(4):
-        for near in range(4):
-            source = here ^ (4 * far + near)
-            core = source & 1
-            half = (source >> 1) & 1
-            block = core * 4 + (source >> 2)
-            if near == 0:
-                values = along[far][0:rows, :]
-            else:
-                values = across[near][far * rows : (far + 1) * rows, :]
-            for pair in range(pairs):
-                real = values[2 * pair : 2 * pair + 1]
-                imag = values[2 * pair + 1 : 2 * pair + 2]
-                size = jnp.sqrt(real * real + imag * imag)
-                target = pl.ds(pl.multiple_of(pair * PATCH + block * 8, 8), 8)
-                field_ref[half, target, :] = jnp.where(
-                    inside, jnp.broadcast_to(real, (8, LANES)), 0.0
-                )
-                field_ref[2 + half, target, :] = jnp.where(
-                    inside, jnp.broadcast_to(imag, (8, LANES)), 0.0
-                )
-                size_ref[half, target, :] = jnp.where(
-                    inside, jnp.broadcast_to(size, (8, LANES)), 0.0
+    for source in range(ratio_ref.shape[0]):
+        core = source & 1
+        half = (source >> 1) & 1
+        block = core * 4 + (source >> 2)
+        values = ratio_ref[source]
+        for pair in range(pairs):
+            real = values[2 * pair : 2 * pair + 1]
+            imag = values[2 * pair + 1 : 2 * pair + 2]
+            size = jnp.sqrt(real * real + imag * imag)
+            start = pair * PATCH + block * 8
+            for target, index, row in (
+                (field_ref, half, real),
+                (field_ref, 2 + half, imag),
+                (size_ref, half, size),
+            ):
+                target[index, start : start + 8, :] = jnp.where(
+                    inside, jnp.broadcast_to(row, (8, LANES)), 0.0
                 )
     for pair in range(pairs):
         lines = slice(pair * PATCH, (pair + 1) * PATCH)
@@ -437,7 +429,6 @@
     pair_total = pairs_here * total
     dates = dates_here * depth
     group = lax.axis_index("date")
-    here = lax.axis_index(("date", "rng", "az"))
     names = ("date", "rng", "az")
 
     def swap(values, offset):
@@ -446,33 +437,27 @@
     view = acquisitions.reshape(dates_here, line_count, 2, columns, LANES)
     view = view.transpose(0, 1, 3, 2, 4).reshape(dates_here, line_count * columns * 2, LANES)
 
-    def block(index):
-        return lax.dynamic_slice_in_dim(view, index * rows, rows, 1)
+    def block(source, offset):
+        return lax.dynamic_slice_in_dim(source, (group ^ offset) * rows, rows, 1)
 
     step = across * cores
-    received = {3: swap(block(group ^ 3), 3 * step)}
-    listed = date_pairs.T[None]
-    listed = jnp.concatenate([listed, swap(listed, 1)], 0)
-    late, listed = lax.optimization_barrier((group, listed))
-    received[2] = swap(block(late ^ 2), 2 * step)
-    received[1] = swap(block(late ^ 1), step)
-    own = block(late)
-    offset = 2
-    while offset < total:
-        listed = jnp.concatenate([listed, swap(listed, offset)], 0)
-        offset *= 2
-    pair_list = listed.reshape(pair_total, 2).T.reshape(-1)
+    farthest, rest = lax.optimization_barrier((block(view, 3), view))
+    received = {3: swap(farthest, 3 * step)}
+    for offset in (1, 2):
+        received[offset] = swap(block(rest, offset), offset * step)
+    own = block(rest, 0)
+    listed = jnp.broadcast_to(date_pairs.reshape(1, -1), (total, 2 * pairs_here))
+    pair_list = lax.all_to_all(listed, names, 0, 0, tiled=True)
     width = look_lines * LANES
     slots = pair_total + dates // 2
     vmem = pl.BlockSpec(memory_space=pltpu.VMEM)
     smem = pl.BlockSpec(memory_space=pltpu.SMEM)
-    piece = jax.ShapeDtypeStruct((2 * pair_total // depth, cells), jnp.float32)
-    pieces = pl.pallas_call(
+    ratios = pl.pallas_call(
         products_kernel,
         name="products",
-        out_shape=[piece] * depth,
+        out_shape=jax.ShapeDtypeStruct((total, 2 * pairs_here, cells), jnp.float32),
         in_specs=[smem, smem] + [vmem] * 5,
-        out_specs=[vmem] * depth,
+        out_specs=vmem,
         scratch_shapes=[
             pltpu.VMEM((dates, 2, look_lines, 8, LANES), jnp.float32),
             pltpu.VMEM((dates, 2, look_lines, 8, LANES), jnp.float32),
@@ -492,15 +477,7 @@
         received[3],
         jnp.asarray(window_table(cells, look_samples, columns)),
     )
-    arrived = [pieces[0]] + [None] * (depth - 1)
-    for k in (3, 2, 1):
-        arrived[k] = swap(pieces[k], k * step)
-    each = 2 * pairs_here
-    sideways = []
-    for k in (3, 2, 1):
-        payload = jnp.concatenate([a[k * each : (k + 1) * each] for a in arrived], 0)
-        sideways.append(swap(payload, k))
-    sideways = sideways[::-1]
+    arrived = lax.all_to_all(ratios, names, 0, 0, tiled=True)
     sample_table, place_table = sample_tables(cells, look_samples, across)
     line_table, end_table = line_tables()
     tables = []
@@ -513,14 +490,14 @@
             jax.ShapeDtypeStruct((pairs_here, 2, HALF, PATCH), jnp.bfloat16),
             jax.ShapeDtypeStruct((pairs_here, HALF, PATCH), jnp.bfloat16),
         ],
-        in_specs=[smem] + [vmem] * (depth + 3 + len(tables)),
+        in_specs=[vmem] * (1 + len(tables)),
         out_specs=[vmem, vmem],
         scratch_shapes=[
             pltpu.VMEM((4, pairs_here * PATCH, cells), jnp.float32),
             pltpu.VMEM((2, pairs_here * PATCH, cells), jnp.float32),
         ],
         compiler_params=pltpu.CompilerParams(vmem_limit_bytes=8 << 20),
-    )(here.reshape(1), *arrived, *sideways, *[jnp.asarray(t) for t in tables])
+    )(arrived, *[jnp.asarray(t) for t in tables])
     return (filtered.transpose(0, 1, 3, 2), coherence.transpose(0, 2, 1))
 
 

time: 41.3 us -> 37.5 us (0.908)
  blocking collectives: 0 us -> 23.1 us
  waiting for transfers between devices: 15.2 us -> 0.01 us
  starting transfers between devices: 17.4 us -> 5.71 us
    all_to_all x0 -> x2, blocking collectives: none -> 23.1 us  [the longest x1 12.7 us: fast_local(): pair_list = lax.all_to_all(listed, names, 0, 0, tiled=True)]
    ppermute x13 -> x3, waiting for transfers between devices: 15.2 us -> 0.01 us  [swap(): return lax.ppermute(values, names, [(i, i ^ offset) for i in range(total)])]
    ppermute x13 -> x3, starting transfers between devices: 17.4 us -> 5.71 us  [swap(): return lax.ppermute(values, names, [(i, i ^ offset) for i in range(total)])]
    dynamic_slice x1 -> x2, local copies, waits for them, and re-layouts: 1.18 us -> 2.05 us  [block(): return lax.dynamic_slice_in_dim(source, (group ^ offset) * rows, rows, 1)]
    unnamed x22, local copies, waits for them, and re-layouts: 0.72 us -> 0.07 us
  transfers between devices with their start and end apart: 13 -> 3, of which waited for: 6 -> 0; matrix products, arithmetic and copies ran while one was open for 4% -> 0% of each run, Pallas kernels for 0% -> 0%
where the time goes in v1:
time: 37.5 us; the launch traced here: 37.2 us
  blocking collectives  23.1 us (62%)
  starting transfers between devices  5.71 us (15%)
  Pallas kernels  5.31 us (14%)
  local copies, waits for them, and re-layouts  2.21 us (6%)
  between operations  0.82 us (2%)
    all_to_all x1, blocking collectives, fast_local(): pair_list = lax.all_to_all(listed, names, 0, 0, tiled=True)  12.7 us
    all_to_all x1, blocking collectives, fast_local(): arrived = lax.all_to_all(ratios, names, 0, 0, tiled=True)  10.4 us
    ppermute x3, starting transfers between devices, swap(): return lax.ppermute(values, names, [(i, i ^ offset) for i in range(total)])  5.71 us
    pallas_call x1, Pallas kernels, fast_local(): pl.pallas_call(products_kernel, name='products', out_shape=jax.ShapeDtype...  3.05 us
    pallas_call x1, Pallas kernels, fast_local(): pl.pallas_call(filter_kernel, name='filter', out_shape=[jax.ShapeDtypeStr...  2.27 us
    dynamic_slice x2, local copies, waits for them, and re-layouts, block(): return lax.dynamic_slice_in_dim(source, (group ^ offset) * rows, rows, 1)  2.05 us
  transfers between devices with their start and end apart: 3, of which 0 were waited for; matrix products, arithmetic and copies ran while one was open for 0% of the time, Pallas kernels for 0%

profile of v1, /device:TPU:0, one launch (start us, length us, event | category | flops | bytes accessed | tf_op | source)
XLA Modules:
  0.0 37.2 jit_solution(14100843387199505698)
XLA Ops:
  0.6 0.9 %constant_dynamic-slice_fusion.3 = bf16[4,128,128]{2,1,0:T(8,128)(2,1)S(1)} fusion(bf16[4,512,128]{2,1,0:T(8,128)(2,1)} %bitcast.10, s32[]{:T(128)S(6)} %select_n.12), kind=kLoop, calls=%fused_computation.3 | loop fusion | bytes 262148 | tf_op jit(solution)/shard_map/dynamic_slice | solution.py:441
  1.6 0.0 copy-start.2
  1.6 0.0 copy-start.5
  1.6 0.0 copy-start.6
  1.6 1.1 %constant_dynamic-slice_fusion = (bf16[4,128,128]{2,1,0:T(8,128)(2,1)S(1)}, bf16[4,128,128]{2,1,0:T(8,128)(2,1)S(1)}, bf16[4,128,128]{2,1,0:T(8,128)(2,1)S(1)}) fusion(bf16[4,512,128]{2,1,0:T(8,128)(2,1)} %bitcast.11, s32[]{:T(128)S(6)} %select_n.15, s32[]{:T(128)S(6)} %select_n.14, s32[]{:T(128)S(6)} %select_n.13), kind=kLoop, calls=%fused_computation | loop fusion | bytes 786444 | tf_op jit(solution)/shard_map/dynamic_slice | solution.py:441
  2.7 0.0 copy-start.10
  2.8 3.1 %collective-permute-start = (bf16[4,128,128]{2,1,0:T(8,128)(2,1)S(1)}, bf16[4,128,128]{2,1,0:T(8,128)(2,1)S(1)}, u32[]{:S(2)}, u32[]{:S(2)}) collective-permute-start(bf16[4,128,128]{2,1,0:T(8,128)(2,1)S(1)} %get-tuple-element.11), channel_id=1, source_target_pairs={{0,4},{1,5},{2,6},{3,7},{4,0},{5,1},{6,2},{7,3},{8,12},{9,13},{10,... | collective-permute-start | bytes 393224 | tf_op jit(solution)/shard_map/ppermute | solution.py:435
  5.9 2.6 %collective-permute-start.1 = (bf16[4,128,128]{2,1,0:T(8,128)(2,1)S(1)}, bf16[4,128,128]{2,1,0:T(8,128)(2,1)S(1)}, u32[]{:S(2)}, u32[]{:S(2)}) collective-permute-start(bf16[4,128,128]{2,1,0:T(8,128)(2,1)S(1)} %get-tuple-element.10), channel_id=1, source_target_pairs={{0,8},{1,9},{2,10},{3,11},{4,12},{5,13},{6,14},{7,15},{8,0},{9,1},... | collective-permute-start | bytes 393224 | tf_op jit(solution)/shard_map/ppermute | solution.py:435
  8.5 0.0 collective-permute-start.2
  8.5 0.0 copy-done.10
  8.5 0.1 broadcast_in_dim.7
  8.6 12.7 %all_to_all.13 = s32[16,1,4]{2,1,0:T(1,128)S(1)} all-to-all(s32[16,1,4]{2,1,0:T(1,128)S(1)} %broadcast_in_dim.8), channel_id=1, replica_groups=mesh['tile'=2,'date'=4,'rng'=2,'az'=2] {'date','rng','az'}, dimensions={0} | all-to-all | bytes 512 | tf_op jit(solution)/shard_map/all_to_all | solution.py:450
  21.3 0.0 collective-permute-done.near_ref
  21.3 0.0 collective-permute-done.1.far_ref
  21.3 0.0 collective-permute-done.2.last_ref
  21.3 0.0 copy-done.2
  21.3 0.0 copy-start
  21.3 0.0 copy-start.1
  21.3 0.0 copy-start.3
  21.3 0.0 copy-start.4
  21.3 3.0 %products.1 = f32[16,4,128]{2,1,0:T(4,128)S(1)} custom-call(s32[1]{0:T(128)} %bitcast.place_ref, s32[16,4]{1,0:T(8,128)S(1)} %bitcast.9, bf16[4,128,128]{2,1,0:T(8,128)(2,1)S(1)} %get-tuple-element.12.own_ref, bf16[4,128,128]{2,1,0:T(8,128)(2,1)S(1)} %collective-permute-done.near_ref, bf16[4,128,128]{2,1,0:T(8,128)(2,1)S(1)} %collective-permute-done.1.far_ref, ...), custom_call_target="tpu_custom_call" | custom-call | tf_op jit(solution)/shard_map/products/pallas_call | solution.py:455
  24.4 0.0 copy-start.7
  24.4 0.0 copy-start.8
  24.4 0.0 copy-start.9
  24.4 10.4 %all_to_all.14.ratio_ref = f32[16,4,128]{2,1,0:T(4,128)S(1)} all-to-all(f32[16,4,128]{2,1,0:T(4,128)S(1)} %products.1), channel_id=1, replica_groups=mesh['tile'=2,'date'=4,'rng'=2,'az'=2] {'date','rng','az'}, dimensions={0} | all-to-all | bytes 65536 | tf_op jit(solution)/shard_map/all_to_all | solution.py:480
  34.9 0.0 copy-done.5
  34.9 0.0 copy-done.6
  34.9 0.0 copy-done
  34.9 0.0 copy-done.1
  34.9 0.0 copy-done.3
  34.9 0.0 copy-done.4
  34.9 0.0 copy-done.7
  34.9 0.0 copy-done.8
  34.9 0.0 copy-done.9
  34.9 2.3 %filter.1 = (bf16[2,2,32,64]{3,2,1,0:T(8,128)(2,1)}, bf16[2,32,64]{2,1,0:T(8,128)(2,1)}) custom-call(f32[16,4,128]{2,1,0:T(4,128)S(1)} %all_to_all.14.ratio_ref, bf16[4,128,256]{2,1,0:T(8,128)(2,1)S(1)} %copy-done, bf16[4,128,256]{2,1,0:T(8,128)(2,1)S(1)} %copy-done.1, bf16[2,32,128]{2,1,0:T(8,128)(2,1)S(1)} %copy-done.7, bf16[64,64]{1,0:T(8,128)(2,1)S(1)} %copy-done.8, ...), custom_call_target="tpu_custom_call" | custom-call | tf_op jit(solution)/shard_map/filter/pallas_call | solution.py:486
  (1 shorter events, 0.0 us)
Async XLA Ops:
  1.6 19.7 %copy-start.2 = (bf16[1024,128]{1,0:T(8,128)(2,1)S(1)}, bf16[1024,128]{1,0:T(8,128)(2,1)}, u32[]{:S(2)}) copy-start(bf16[1024,128]{1,0:T(8,128)(2,1)} %constant.37.clone.window_ref) | copy-start | bytes 786436
  1.6 33.3 %copy-start.5 = (bf16[512,64]{1,0:T(8,128)(2,1)S(1)}, bf16[512,64]{1,0:T(8,128)(2,1)}, u32[]{:S(2)}) copy-start(bf16[512,64]{1,0:T(8,128)(2,1)} %constant.45.clone.end_high_ref) | copy-start | bytes 196612
  1.6 33.3 %copy-start.6 = (bf16[512,64]{1,0:T(8,128)(2,1)S(1)}, bf16[512,64]{1,0:T(8,128)(2,1)}, u32[]{:S(2)}) copy-start(bf16[512,64]{1,0:T(8,128)(2,1)} %constant.46.clone.end_low_ref) | copy-start | bytes 196612
  2.7 5.7 %copy-start.10 = (s32[2,2]{1,0:T(2,128)S(1)}, s32[2,2]{1,0:T(2,128)}, u32[]{:S(2)}) copy-start(s32[2,2]{1,0:T(2,128)} %param.13) | copy-start | bytes 52
  2.8 18.5 %collective-permute-start = (bf16[4,128,128]{2,1,0:T(8,128)(2,1)S(1)}, bf16[4,128,128]{2,1,0:T(8,128)(2,1)S(1)}, u32[]{:S(2)}, u32[]{:S(2)}) collective-permute-start(bf16[4,128,128]{2,1,0:T(8,128)(2,1)S(1)} %get-tuple-element.11), channel_id=1, source_target_pairs={{0,4},{1,5},{2,6},{3,7},{4,0},{5,1},{6,2},{7,3},{8,12},{9,13},{10,... | collective-permute-start | bytes 393224 | tf_op jit(solution)/shard_map/ppermute | solution.py:435
  5.9 15.4 %collective-permute-start.1 = (bf16[4,128,128]{2,1,0:T(8,128)(2,1)S(1)}, bf16[4,128,128]{2,1,0:T(8,128)(2,1)S(1)}, u32[]{:S(2)}, u32[]{:S(2)}) collective-permute-start(bf16[4,128,128]{2,1,0:T(8,128)(2,1)S(1)} %get-tuple-element.10), channel_id=1, source_target_pairs={{0,8},{1,9},{2,10},{3,11},{4,12},{5,13},{6,14},{7,15},{8,0},{9,1},... | collective-permute-start | bytes 393224 | tf_op jit(solution)/shard_map/ppermute | solution.py:435
  8.5 12.8 %collective-permute-start.2 = (bf16[4,128,128]{2,1,0:T(8,128)(2,1)S(1)}, bf16[4,128,128]{2,1,0:T(8,128)(2,1)S(1)}, u32[]{:S(2)}, u32[]{:S(2)}) collective-permute-start(bf16[4,128,128]{2,1,0:T(8,128)(2,1)S(1)} %constant_dynamic-slice_fusion.3), channel_id=1, source_target_pairs={{0,12},{1,13},{2,14},{3,15},{4,8},{5,9},{6,10},{7,11},{8,4},{9,5},... | collective-permute-start | bytes 393224 | tf_op jit(solution)/shard_map/ppermute | solution.py:435
  21.3 13.6 %copy-start = (bf16[4,128,256]{2,1,0:T(8,128)(2,1)S(1)}, bf16[4,128,256]{2,1,0:T(8,128)(2,1)}, u32[]{:S(2)}) copy-start(bf16[4,128,256]{2,1,0:T(8,128)(2,1)} %constant.38.clone.sample_high_ref) | copy-start | bytes 786436
  21.3 13.6 %copy-start.1 = (bf16[4,128,256]{2,1,0:T(8,128)(2,1)S(1)}, bf16[4,128,256]{2,1,0:T(8,128)(2,1)}, u32[]{:S(2)}) copy-start(bf16[4,128,256]{2,1,0:T(8,128)(2,1)} %constant.39.clone.sample_low_ref) | copy-start | bytes 786436
  21.3 13.6 %copy-start.3 = (bf16[256,256]{1,0:T(8,128)(2,1)S(1)}, bf16[256,256]{1,0:T(8,128)(2,1)}, u32[]{:S(2)}) copy-start(bf16[256,256]{1,0:T(8,128)(2,1)} %constant.43.clone.back_high_ref) | copy-start | bytes 393220
  21.3 13.6 %copy-start.4 = (bf16[256,256]{1,0:T(8,128)(2,1)S(1)}, bf16[256,256]{1,0:T(8,128)(2,1)}, u32[]{:S(2)}) copy-start(bf16[256,256]{1,0:T(8,128)(2,1)} %constant.44.clone.back_low_ref) | copy-start | bytes 393220
  24.4 10.5 %copy-start.7 = (bf16[2,32,128]{2,1,0:T(8,128)(2,1)S(1)}, bf16[2,32,128]{2,1,0:T(8,128)(2,1)}, u32[]{:S(2)}) copy-start(bf16[2,32,128]{2,1,0:T(8,128)(2,1)} %constant.40.clone.place_table_ref) | copy-start | bytes 49156
  24.4 10.5 %copy-start.8 = (bf16[64,64]{1,0:T(8,128)(2,1)S(1)}, bf16[64,64]{1,0:T(8,128)(2,1)}, u32[]{:S(2)}) copy-start(bf16[64,64]{1,0:T(8,128)(2,1)} %constant.41.clone.line_high_ref) | copy-start | bytes 24580
  24.4 10.5 %copy-start.9 = (bf16[64,64]{1,0:T(8,128)(2,1)S(1)}, bf16[64,64]{1,0:T(8,128)(2,1)}, u32[]{:S(2)}) copy-start(bf16[64,64]{1,0:T(8,128)(2,1)} %constant.42.clone.line_low_ref) | copy-start | bytes 24580

commit v2 on v1

--- a/solution.py
+++ b/solution.py
@@ -191,16 +191,10 @@
     return (high, low)
 
 
-def window_table(cells, samples, columns):
+def window_table(cells):
     lane = np.arange(LANES)
-    out = np.zeros((cells // samples, LANES, cells), np.float32)
-    cell = np.arange(cells)
-    per_column = samples // columns
-    for line in range(cells // samples):
-        out[line] = (lane[:, None] // LOOK_RG == cell[None, :] % per_column) & (
-            cell[None, :] // samples == line
-        )
-    return out.reshape(-1, cells).astype(jnp.bfloat16)
+    table = lane[:, None] // LOOK_RG == np.arange(cells)[None, :] % (LANES // LOOK_RG)
+    return np.concatenate([table, table], 0).astype(np.float32).astype(jnp.bfloat16)
 
 
 def sample_tables(cells, samples, halves):
@@ -215,7 +209,10 @@
         place.append(np.arange(halves * samples)[:, None] == position[None, :])
     real = [np.concatenate([c, -s, -s, -c], 1) for c, s in forward]
     imag = [np.concatenate([s, c, c, -s], 1) for c, s in forward]
-    return (np.stack(real + imag), np.stack(place).astype(np.float32).astype(jnp.bfloat16))
+    return (
+        np.concatenate(real + imag, 0),
+        np.concatenate(place, 1).astype(np.float32).astype(jnp.bfloat16),
+    )
 
 
 def line_tables():
@@ -261,123 +258,144 @@
 def products_kernel(
     place_ref, pair_ref, own_ref, near_ref, far_ref, last_ref, window_ref,
     out_ref,
-    plain_ref, turned_ref, high_ref, low_ref, sum_ref, root_ref, scale_ref,
+    part_ref, split_ref, power_ref, sum_ref, date_ref, root_ref, scale_ref,
 ):
     group = place_ref[0]
     dates_here = own_ref.shape[0]
-    dates = plain_ref.shape[0]
-    looks = plain_ref.shape[2]
+    dates = part_ref.shape[0]
     owners = pair_ref.shape[0]
     pairs_here = pair_ref.shape[1] // 2
     pair_total = owners * pairs_here
-    even = lax.broadcasted_iota(jnp.int32, (looks, 8, LANES), 1) % 2 == 0
+    row = lax.broadcasted_iota(jnp.int32, (8, LANES), 0)
+    low = row < 4
+    even = row % 2 == 0
+
+    def split(target, slot, first, second):
+        high, rest = rounded_parts(jnp.concatenate([first, second], axis=0))
+        target[slot, :, :LANES] = high
+        target[slot, :, LANES:] = rest
+
+    def total(terms):
+        while len(terms) > 1:
+            terms = [a + b for a, b in zip(terms[::2], terms[1::2])]
+        return terms[0]
+
     for offset, ref in enumerate((own_ref, near_ref, far_ref, last_ref)):
         base = (group ^ offset) * dates_here
         for index in range(dates_here):
-            values = ref[index].astype(jnp.float32).reshape(looks, 2, 8, LANES)
-            for part in range(2):
-                lines = values[:, part]
-                plain_ref[base + index, part] = lines
-                turned_ref[base + index, part] = jnp.where(
-                    even, -pltpu.roll(lines, 7, 1), pltpu.roll(lines, 1, 1)
-                )
-
-    def keep(slot, first, second):
-        joined = jnp.concatenate([first, second], axis=1)
-        high, low = rounded_parts(joined)
-        for look in range(looks):
-            columns = slice(look * LANES, (look + 1) * LANES)
-            high_ref[slot, :, columns] = high[look]
-            low_ref[slot, :, columns] = low[look]
-
-    def one_pair(index, carry):
-        owner = index // pairs_here
-        earlier = pair_ref[owner, index % pairs_here]
-        later = pair_ref[owner, pairs_here + index % pairs_here]
-        left0 = plain_ref[earlier, 0]
-        left1 = plain_ref[earlier, 1]
-        real = left0 * plain_ref[later, 0] + left1 * plain_ref[later, 1]
-        imag = left0 * turned_ref[later, 0] + left1 * turned_ref[later, 1]
-        keep(index, real, imag)
+            values = ref[index].astype(jnp.float32).reshape(8, 2, 8, LANES)
+            for pick in range(2):
+                squares = []
+                for part in range(2):
+                    lines = []
+                    for look in (pick, pick + 2):
+                        upper, lower = values[look, part], values[look + 4, part]
+                        lines.append(
+                            (
+                                jnp.where(low, upper, pltpu.roll(lower, 4, 0)),
+                                jnp.where(low, pltpu.roll(upper, 4, 0), lower),
+                            )
+                        )
+                    for line in range(2):
+                        first, second = lines[0][line], lines[1][line]
+                        real = jnp.where(even, first, pltpu.roll(second, 1, 0))
+                        imag = jnp.where(even, pltpu.roll(first, 7, 0), second)
+                        part_ref[base + index, 0, pick, 2 * part + line] = real
+                        part_ref[base + index, 1, pick, 2 * part + line] = imag
+                        squares += [real * real, imag * imag]
+                high, rest = rounded_parts(total(squares))
+                power_ref[base + index, 8 * pick : 8 * pick + 8, :LANES] = high
+                power_ref[base + index, 8 * pick : 8 * pick + 8, LANES:] = rest
+
+    def one_owner(owner, carry):
+        for index in range(pairs_here):
+            earlier = pair_ref[owner, index]
+            later = pair_ref[owner, pairs_here + index]
+            real, imag = [], []
+            for pick in range(2):
+                dot_terms, cross_terms = [], []
+                for line in range(LOOK_AZ):
+                    left_real = part_ref[earlier, 0, pick, line]
+                    left_imag = part_ref[earlier, 1, pick, line]
+                    right_real = part_ref[later, 0, pick, line]
+                    right_imag = part_ref[later, 1, pick, line]
+                    dot_terms += [left_real * right_real, left_imag * right_imag]
+                    cross_terms += [left_imag * right_real - left_real * right_imag]
+                real.append(total(dot_terms))
+                imag.append(total(cross_terms))
+            slot = 2 * (owner * pairs_here + index)
+            split(split_ref, slot, *real)
+            split(split_ref, slot + 1, *imag)
         return carry
 
-    def two_dates(index, carry):
-        def power(date):
-            return plain_ref[date, 0] * plain_ref[date, 0] + plain_ref[date, 1] * plain_ref[date, 1]
-
-        keep(pair_total + index, power(2 * index), power(2 * index + 1))
-        return carry
-
-    lax.fori_loop(0, dates // 2, two_dates, 0)
-    lax.fori_loop(0, pair_total, one_pair, 0)
-    rows = high_ref.shape[0] * 16
-    width = high_ref.shape[2]
+    lax.fori_loop(0, owners, one_owner, 0, unroll=2)
     table = window_ref[...]
-    sum_ref[...] = dot(high_ref[...].reshape(rows, width), table) + dot(
-        low_ref[...].reshape(rows, width), table
-    )
+    date_ref[...] = dot(power_ref[...].reshape(16 * dates, 2 * LANES), table)
+    sum_ref[...] = dot(split_ref[...].reshape(32 * pair_total, 2 * LANES), table)
     share = 1.0 / (LOOK_AZ * LOOK_RG)
 
-    def fold(start, count):
-        def added(picks):
-            total = sum_ref[pl.ds(start * 8 + picks[0], count, stride=8), :]
-            for pick in picks[1:]:
-                total = total + sum_ref[pl.ds(start * 8 + pick, count, stride=8), :]
-            return total
-
-        second = lax.broadcasted_iota(jnp.int32, (count, LANES), 1) // 8 % 2 == 1
-        return jnp.where(second, added((2, 3, 6, 7)), added((0, 1, 4, 5))) * share
-
-    root_ref[...] = lax.rsqrt(fold(2 * pair_total, dates) + EPSILON)
+    def fold(ref, count):
+        lane = lax.broadcasted_iota(jnp.int32, (count, LANES), 1)
+        look = lane // 16
+        source = look % 2 * 8 + look // 4 * 4 + lane // 8 % 2 * 2 + look // 2 % 2
+        out = ref[pl.ds(0, count, stride=16), :]
+        for pick in range(1, 16):
+            out = jnp.where(source == pick, ref[pl.ds(pick, count, stride=16), :], out)
+        return out * share
+
+    root_ref[...] = lax.rsqrt(fold(date_ref, dates) + EPSILON)
     for owner in range(owners):
         for index in range(pairs_here):
             earlier = root_ref[pl.ds(pair_ref[owner, index], 1), :]
             later = root_ref[pl.ds(pair_ref[owner, pairs_here + index], 1), :]
             start = 2 * (owner * pairs_here + index)
             scale_ref[start : start + 2, :] = jnp.broadcast_to(earlier * later, (2, LANES))
-    ratio = fold(0, 2 * pair_total) * scale_ref[...]
+    ratio = fold(sum_ref, 2 * pair_total) * scale_ref[...]
     out_ref[...] = ratio.reshape(out_ref.shape)
 
 
 def filter_kernel(
     ratio_ref, sample_high_ref, sample_low_ref, place_table_ref, line_high_ref, line_low_ref,
     back_high_ref, back_low_ref, end_high_ref, end_low_ref,
-    filtered_ref, coherence_ref, field_ref, size_ref,
+    filtered_ref, coherence_ref, high_ref, low_ref, size_ref,
 ):
     pairs = coherence_ref.shape[0]
     lane = lax.broadcasted_iota(jnp.int32, (8, LANES), 1)
     line = lax.broadcasted_iota(jnp.int32, (8, LANES), 0)
     inside = lane // 16 == line
-    for source in range(ratio_ref.shape[0]):
+    sources = ratio_ref.shape[0]
+    values = ratio_ref[...].reshape(sources * 2 * pairs, LANES)
+    square = values * values
+    size = jnp.sqrt(square + pltpu.roll(square, square.shape[0] - 1, 0))
+
+    def place(target, start, column, row):
+        target[start : start + 8, column * LANES : (column + 1) * LANES] = jnp.where(
+            inside, jnp.broadcast_to(row, (8, LANES)), 0.0
+        ).astype(target.dtype)
+
+    high = values.astype(jnp.bfloat16).astype(jnp.float32)
+    low = values - high
+    for source in range(sources):
         core = source & 1
         half = (source >> 1) & 1
         block = core * 4 + (source >> 2)
-        values = ratio_ref[source]
         for pair in range(pairs):
-            real = values[2 * pair : 2 * pair + 1]
-            imag = values[2 * pair + 1 : 2 * pair + 2]
-            size = jnp.sqrt(real * real + imag * imag)
             start = pair * PATCH + block * 8
-            for target, index, row in (
-                (field_ref, half, real),
-                (field_ref, 2 + half, imag),
-                (size_ref, half, size),
-            ):
-                target[index, start : start + 8, :] = jnp.where(
-                    inside, jnp.broadcast_to(row, (8, LANES)), 0.0
-                )
+            first = (source * pairs + pair) * 2
+            for part in range(2):
+                pick = slice(first + part, first + part + 1)
+                place(high_ref, start, 2 * part + half, high[pick])
+                place(low_ref, start, 2 * part + half, low[pick])
+            place(size_ref, start, half, size[first : first + 1])
     for pair in range(pairs):
         lines = slice(pair * PATCH, (pair + 1) * PATCH)
-        magnitude = dot_rows(
-            place_table_ref[0], size_ref[0, lines].astype(jnp.bfloat16)
-        ) + dot_rows(place_table_ref[1], size_ref[1, lines].astype(jnp.bfloat16))
+        magnitude = dot_rows(place_table_ref[...], size_ref[lines])
         coherence_ref[pair] = magnitude.astype(coherence_ref.dtype)
-    spread = None
-    for index in range(4):
-        high, low = rounded_parts(field_ref[index])
-        table = sample_high_ref[index]
-        term = dot(high, table) + dot(low, table) + dot(high, sample_low_ref[index])
-        spread = term if spread is None else spread + term
+    spread = (
+        dot(high_ref[...], sample_high_ref[...])
+        + dot(low_ref[...], sample_high_ref[...])
+        + dot(high_ref[...], sample_low_ref[...])
+    )
     columns = []
     for half in range(2):
         for pair in range(pairs):
@@ -441,15 +459,10 @@
         return lax.dynamic_slice_in_dim(source, (group ^ offset) * rows, rows, 1)
 
     step = across * cores
-    farthest, rest = lax.optimization_barrier((block(view, 3), view))
-    received = {3: swap(farthest, 3 * step)}
-    for offset in (1, 2):
-        received[offset] = swap(block(rest, offset), offset * step)
-    own = block(rest, 0)
+    received = {offset: swap(block(view, offset), offset * step) for offset in (3, 1, 2)}
+    own = block(view, 0)
     listed = jnp.broadcast_to(date_pairs.reshape(1, -1), (total, 2 * pairs_here))
     pair_list = lax.all_to_all(listed, names, 0, 0, tiled=True)
-    width = look_lines * LANES
-    slots = pair_total + dates // 2
     vmem = pl.BlockSpec(memory_space=pltpu.VMEM)
     smem = pl.BlockSpec(memory_space=pltpu.SMEM)
     ratios = pl.pallas_call(
@@ -459,11 +472,11 @@
         in_specs=[smem, smem] + [vmem] * 5,
         out_specs=vmem,
         scratch_shapes=[
-            pltpu.VMEM((dates, 2, look_lines, 8, LANES), jnp.float32),
-            pltpu.VMEM((dates, 2, look_lines, 8, LANES), jnp.float32),
-            pltpu.VMEM((slots, 16, width), jnp.bfloat16),
-            pltpu.VMEM((slots, 16, width), jnp.bfloat16),
-            pltpu.VMEM((slots * 16, cells), jnp.float32),
+            pltpu.VMEM((dates, 2, 2, LOOK_AZ, 8, LANES), jnp.float32),
+            pltpu.VMEM((2 * pair_total, 16, 2 * LANES), jnp.bfloat16),
+            pltpu.VMEM((dates, 16, 2 * LANES), jnp.bfloat16),
+            pltpu.VMEM((32 * pair_total, cells), jnp.float32),
+            pltpu.VMEM((16 * dates, cells), jnp.float32),
             pltpu.VMEM((dates, cells), jnp.float32),
             pltpu.VMEM((2 * pair_total, cells), jnp.float32),
         ],
@@ -475,7 +488,7 @@
         received[1],
         received[2],
         received[3],
-        jnp.asarray(window_table(cells, look_samples, columns)),
+        jnp.asarray(window_table(cells)),
     )
     arrived = lax.all_to_all(ratios, names, 0, 0, tiled=True)
     sample_table, place_table = sample_tables(cells, look_samples, across)
@@ -493,8 +506,9 @@
         in_specs=[vmem] * (1 + len(tables)),
         out_specs=[vmem, vmem],
         scratch_shapes=[
-            pltpu.VMEM((4, pairs_here * PATCH, cells), jnp.float32),
-            pltpu.VMEM((2, pairs_here * PATCH, cells), jnp.float32),
+            pltpu.VMEM((pairs_here * PATCH, 2 * across * cells), jnp.bfloat16),
+            pltpu.VMEM((pairs_here * PATCH, 2 * across * cells), jnp.bfloat16),
+            pltpu.VMEM((pairs_here * PATCH, across * cells), jnp.bfloat16),
         ],
         compiler_params=pltpu.CompilerParams(vmem_limit_bytes=8 << 20),
     )(arrived, *[jnp.asarray(t) for t in tables])

time: 37.5 us -> 35.1 us (0.936)
  Pallas kernels: 5.31 us -> 3.9 us
  local copies, waits for them, and re-layouts: 2.21 us -> 1.39 us
    pallas_call x1, Pallas kernels: 3.05 us -> 1.77 us  [fast_local(): pl.pallas_call(products_kernel, name='products', out_shape=jax.ShapeDtype...]
    dynamic_slice x2 -> x1, local copies, waits for them, and re-layouts: 2.05 us -> 1.23 us  [block(): return lax.dynamic_slice_in_dim(source, (group ^ offset) * rows, rows, 1)]
where the time goes in v2:
time: 35.1 us; the launch traced here: 34.8 us
  blocking collectives  23 us (66%)
  starting transfers between devices  5.71 us (16%)
  Pallas kernels  3.9 us (11%)
  local copies, waits for them, and re-layouts  1.39 us (4%)
  between operations  0.8 us (2%)
    all_to_all x1, blocking collectives, fast_local(): pair_list = lax.all_to_all(listed, names, 0, 0, tiled=True)  12.7 us
    all_to_all x1, blocking collectives, fast_local(): arrived = lax.all_to_all(ratios, names, 0, 0, tiled=True)  10.3 us
    ppermute x3, starting transfers between devices, swap(): return lax.ppermute(values, names, [(i, i ^ offset) for i in range(total)])  5.71 us
    pallas_call x1, Pallas kernels, fast_local(): pl.pallas_call(filter_kernel, name='filter', out_shape=[jax.ShapeDtypeStr...  2.13 us
    pallas_call x1, Pallas kernels, fast_local(): pl.pallas_call(products_kernel, name='products', out_shape=jax.ShapeDtype...  1.77 us
    dynamic_slice x1, local copies, waits for them, and re-layouts, block(): return lax.dynamic_slice_in_dim(source, (group ^ offset) * rows, rows, 1)  1.23 us
  transfers between devices with their start and end apart: 3, of which 0 were waited for; matrix products, arithmetic and copies ran while one was open for 0% of the time, Pallas kernels for 0%

profile of v2, /device:TPU:0, one launch (start us, length us, event | category | flops | bytes accessed | tf_op | source)
XLA Modules:
  0.0 34.8 jit_solution(3862122993042187114)
XLA Ops:
  0.7 0.0 copy-start.6
  0.7 0.0 copy-start.3
  0.7 0.0 copy-start.4
  0.7 0.0 copy-start.5
  0.7 1.2 %constant_dynamic-slice_fusion = (bf16[4,128,128]{2,1,0:T(8,128)(2,1)S(1)}, bf16[4,128,128]{2,1,0:T(8,128)(2,1)S(1)}, bf16[4,128,128]{2,1,0:T(8,128)(2,1)S(1)}, bf16[4,128,128]{2,1,0:T(8,128)(2,1)S(1)}) fusion(bf16[4,512,128]{2,1,0:T(8,128)(2,1)} %bitcast.10, s32[]{:T(128)S(6)} %select_n.15, s32[]{:T(128)S(6)} %select_n.14, s32[]{:T(128)S(6)} %select_n.13, ...), kind=kLoop, calls=%fused_computation | loop fusion | bytes 1048592 | tf_op jit(solution)/shard_map/dynamic_slice | solution.py:459
  1.9 3.1 %collective-permute-start = (bf16[4,128,128]{2,1,0:T(8,128)(2,1)S(1)}, bf16[4,128,128]{2,1,0:T(8,128)(2,1)S(1)}, u32[]{:S(2)}, u32[]{:S(2)}) collective-permute-start(bf16[4,128,128]{2,1,0:T(8,128)(2,1)S(1)} %get-tuple-element.8), channel_id=1, source_target_pairs={{0,4},{1,5},{2,6},{3,7},{4,0},{5,1},{6,2},{7,3},{8,12},{9,13},{10,... | collective-permute-start | bytes 393224 | tf_op jit(solution)/shard_map/ppermute | solution.py:453
  5.1 0.0 copy-start.10
  5.1 2.6 %collective-permute-start.1 = (bf16[4,128,128]{2,1,0:T(8,128)(2,1)S(1)}, bf16[4,128,128]{2,1,0:T(8,128)(2,1)S(1)}, u32[]{:S(2)}, u32[]{:S(2)}) collective-permute-start(bf16[4,128,128]{2,1,0:T(8,128)(2,1)S(1)} %get-tuple-element.7), channel_id=1, source_target_pairs={{0,8},{1,9},{2,10},{3,11},{4,12},{5,13},{6,14},{7,15},{8,0},{9,1},... | collective-permute-start | bytes 393224 | tf_op jit(solution)/shard_map/ppermute | solution.py:453
  7.6 0.0 collective-permute-start.2
  7.6 0.0 copy-done.10
  7.6 0.1 broadcast_in_dim.7
  7.7 0.0 copy-start.9
  7.7 12.7 %all_to_all.13 = s32[16,1,4]{2,1,0:T(1,128)S(1)} all-to-all(s32[16,1,4]{2,1,0:T(1,128)S(1)} %broadcast_in_dim.8), channel_id=1, replica_groups=mesh['tile'=2,'date'=4,'rng'=2,'az'=2] {'date','rng','az'}, dimensions={0} | all-to-all | bytes 512 | tf_op jit(solution)/shard_map/all_to_all | solution.py:465
  20.4 0.0 collective-permute-done.near_ref
  20.4 0.0 collective-permute-done.1.far_ref
  20.5 0.0 collective-permute-done.2.last_ref
  20.5 0.0 copy-done.6
  20.5 0.0 copy-start
  20.5 0.0 copy-start.1
  20.5 0.0 copy-start.2
  20.5 1.8 %products.1 = f32[16,4,128]{2,1,0:T(4,128)S(1)} custom-call(s32[1]{0:T(128)} %bitcast.place_ref, s32[16,4]{1,0:T(8,128)S(1)} %bitcast.9, bf16[4,128,128]{2,1,0:T(8,128)(2,1)S(1)} %get-tuple-element.9.own_ref, bf16[4,128,128]{2,1,0:T(8,128)(2,1)S(1)} %collective-permute-done.near_ref, bf16[4,128,128]{2,1,0:T(8,128)(2,1)S(1)} %collective-permute-done.1.far_ref, ...), custom_call_target="tpu_custom_call" | custom-call | tf_op jit(solution)/shard_map/products/pallas_call | solution.py:468
  22.3 0.0 copy-start.7
  22.3 0.0 copy-start.8
  22.3 10.3 %all_to_all.14.ratio_ref = f32[16,4,128]{2,1,0:T(4,128)S(1)} all-to-all(f32[16,4,128]{2,1,0:T(4,128)S(1)} %products.1), channel_id=1, replica_groups=mesh['tile'=2,'date'=4,'rng'=2,'az'=2] {'date','rng','az'}, dimensions={0} | all-to-all | bytes 65536 | tf_op jit(solution)/shard_map/all_to_all | solution.py:493
  32.6 0.0 copy-done.3
  32.6 0.0 copy-done.4
  32.6 0.0 copy-done.5
  32.6 0.0 copy-done.9
  32.6 0.0 copy-done
  32.6 0.0 copy-done.1
  32.7 0.0 copy-done.2
  32.7 0.0 copy-done.7
  32.7 0.0 copy-done.8
  32.7 2.1 %filter.1 = (bf16[2,2,32,64]{3,2,1,0:T(8,128)(2,1)}, bf16[2,32,64]{2,1,0:T(8,128)(2,1)}) custom-call(f32[16,4,128]{2,1,0:T(4,128)S(1)} %all_to_all.14.ratio_ref, bf16[512,256]{1,0:T(8,128)(2,1)S(1)} %copy-done, bf16[512,256]{1,0:T(8,128)(2,1)S(1)} %copy-done.1, bf16[32,256]{1,0:T(8,128)(2,1)S(1)} %copy-done.7, bf16[64,64]{1,0:T(8,128)(2,1)S(1)} %copy-done.8, ...), custom_call_target="tpu_custom_call" | custom-call | tf_op jit(solution)/shard_map/filter/pallas_call | solution.py:499
  (1 shorter events, 0.0 us)
Async XLA Ops:
  0.7 19.8 %copy-start.6 = (bf16[256,128]{1,0:T(8,128)(2,1)S(1)}, bf16[256,128]{1,0:T(8,128)(2,1)}, u32[]{:S(2)}) copy-start(bf16[256,128]{1,0:T(8,128)(2,1)} %constant.37.clone.window_ref) | copy-start | bytes 196612
  0.7 32.0 %copy-start.3 = (bf16[256,256]{1,0:T(8,128)(2,1)S(1)}, bf16[256,256]{1,0:T(8,128)(2,1)}, u32[]{:S(2)}) copy-start(bf16[256,256]{1,0:T(8,128)(2,1)} %constant.44.clone.back_low_ref) | copy-start | bytes 393220
  0.7 31.9 %copy-start.4 = (bf16[512,64]{1,0:T(8,128)(2,1)S(1)}, bf16[512,64]{1,0:T(8,128)(2,1)}, u32[]{:S(2)}) copy-start(bf16[512,64]{1,0:T(8,128)(2,1)} %constant.45.clone.end_high_ref) | copy-start | bytes 196612
  0.7 31.9 %copy-start.5 = (bf16[512,64]{1,0:T(8,128)(2,1)S(1)}, bf16[512,64]{1,0:T(8,128)(2,1)}, u32[]{:S(2)}) copy-start(bf16[512,64]{1,0:T(8,128)(2,1)} %constant.46.clone.end_low_ref) | copy-start | bytes 196612
  1.9 18.5 %collective-permute-start = (bf16[4,128,128]{2,1,0:T(8,128)(2,1)S(1)}, bf16[4,128,128]{2,1,0:T(8,128)(2,1)S(1)}, u32[]{:S(2)}, u32[]{:S(2)}) collective-permute-start(bf16[4,128,128]{2,1,0:T(8,128)(2,1)S(1)} %get-tuple-element.8), channel_id=1, source_target_pairs={{0,4},{1,5},{2,6},{3,7},{4,0},{5,1},{6,2},{7,3},{8,12},{9,13},{10,... | collective-permute-start | bytes 393224 | tf_op jit(solution)/shard_map/ppermute | solution.py:453
  5.1 2.6 %copy-start.10 = (s32[2,2]{1,0:T(2,128)S(1)}, s32[2,2]{1,0:T(2,128)}, u32[]{:S(2)}) copy-start(s32[2,2]{1,0:T(2,128)} %param.13) | copy-start | bytes 52
  5.1 15.4 %collective-permute-start.1 = (bf16[4,128,128]{2,1,0:T(8,128)(2,1)S(1)}, bf16[4,128,128]{2,1,0:T(8,128)(2,1)S(1)}, u32[]{:S(2)}, u32[]{:S(2)}) collective-permute-start(bf16[4,128,128]{2,1,0:T(8,128)(2,1)S(1)} %get-tuple-element.7), channel_id=1, source_target_pairs={{0,8},{1,9},{2,10},{3,11},{4,12},{5,13},{6,14},{7,15},{8,0},{9,1},... | collective-permute-start | bytes 393224 | tf_op jit(solution)/shard_map/ppermute | solution.py:453
  7.6 12.8 %collective-permute-start.2 = (bf16[4,128,128]{2,1,0:T(8,128)(2,1)S(1)}, bf16[4,128,128]{2,1,0:T(8,128)(2,1)S(1)}, u32[]{:S(2)}, u32[]{:S(2)}) collective-permute-start(bf16[4,128,128]{2,1,0:T(8,128)(2,1)S(1)} %get-tuple-element.6), channel_id=1, source_target_pairs={{0,12},{1,13},{2,14},{3,15},{4,8},{5,9},{6,10},{7,11},{8,4},{9,5},... | collective-permute-start | bytes 393224 | tf_op jit(solution)/shard_map/ppermute | solution.py:453
  7.7 24.9 %copy-start.9 = (bf16[64,64]{1,0:T(8,128)(2,1)S(1)}, bf16[64,64]{1,0:T(8,128)(2,1)}, u32[]{:S(2)}) copy-start(bf16[64,64]{1,0:T(8,128)(2,1)} %constant.42.clone.line_low_ref) | copy-start | bytes 24580
  20.5 12.2 %copy-start = (bf16[512,256]{1,0:T(8,128)(2,1)S(1)}, bf16[512,256]{1,0:T(8,128)(2,1)}, u32[]{:S(2)}) copy-start(bf16[512,256]{1,0:T(8,128)(2,1)} %constant.38.clone.sample_high_ref) | copy-start | bytes 786436
  20.5 12.2 %copy-start.1 = (bf16[512,256]{1,0:T(8,128)(2,1)S(1)}, bf16[512,256]{1,0:T(8,128)(2,1)}, u32[]{:S(2)}) copy-start(bf16[512,256]{1,0:T(8,128)(2,1)} %constant.39.clone.sample_low_ref) | copy-start | bytes 786436
  20.5 12.2 %copy-start.2 = (bf16[256,256]{1,0:T(8,128)(2,1)S(1)}, bf16[256,256]{1,0:T(8,128)(2,1)}, u32[]{:S(2)}) copy-start(bf16[256,256]{1,0:T(8,128)(2,1)} %constant.43.clone.back_high_ref) | copy-start | bytes 393220
  22.3 10.4 %copy-start.7 = (bf16[32,256]{1,0:T(8,128)(2,1)S(1)}, bf16[32,256]{1,0:T(8,128)(2,1)}, u32[]{:S(2)}) copy-start(bf16[32,256]{1,0:T(8,128)(2,1)} %constant.40.clone.place_table_ref) | copy-start | bytes 49156
  22.3 10.4 %copy-start.8 = (bf16[64,64]{1,0:T(8,128)(2,1)S(1)}, bf16[64,64]{1,0:T(8,128)(2,1)}, u32[]{:S(2)}) copy-start(bf16[64,64]{1,0:T(8,128)(2,1)} %constant.41.clone.line_high_ref) | copy-start | bytes 24580

commit v3 on v2

--- a/solution.py
+++ b/solution.py
@@ -184,11 +184,16 @@
     return (high, low)
 
 
-def split_table(table):
+def split_table(table, axis):
     table = np.asarray(table, np.float32)
     high = table.astype(jnp.bfloat16)
     low = (table - high.astype(np.float32)).astype(jnp.bfloat16)
-    return (high, low)
+    return np.concatenate([high, high, low], axis)
+
+
+def three_parts(values, axis):
+    high, low = rounded_parts(values)
+    return jnp.concatenate([high, low, high], axis)
 
 
 def window_table(cells):
@@ -207,8 +212,8 @@
         angle = 2.0 * np.pi * (position[:, None] * frequency[None, :] % PATCH) / PATCH
         forward.append((np.cos(angle), np.sin(angle)))
         place.append(np.arange(halves * samples)[:, None] == position[None, :])
-    real = [np.concatenate([c, -s, -s, -c], 1) for c, s in forward]
-    imag = [np.concatenate([s, c, c, -s], 1) for c, s in forward]
+    real = [np.concatenate([c, -s], 1) for c, s in forward]
+    imag = [np.concatenate([s, c], 1) for c, s in forward]
     return (
         np.concatenate(real + imag, 0),
         np.concatenate(place, 1).astype(np.float32).astype(jnp.bfloat16),
@@ -242,7 +247,9 @@
     direct = np.concatenate([np.concatenate([c, -s], 1), np.concatenate([s, c], 1)], 0)
     turned = np.concatenate([np.concatenate([-s, -c], 1), np.concatenate([c, -s], 1)], 0)
     identity = np.eye(pairs)
-    return np.concatenate([np.kron(identity, direct), np.kron(identity, turned)], 0)
+    table = np.concatenate([np.kron(identity, direct), np.kron(identity, turned)], 0)
+    table = table.reshape(-1, pairs, 2, PATCH).transpose(0, 2, 1, 3)
+    return table.reshape(-1, 2 * pairs * PATCH)
 
 
 def dot(left, right):
@@ -328,7 +335,7 @@
             split(split_ref, slot + 1, *imag)
         return carry
 
-    lax.fori_loop(0, owners, one_owner, 0, unroll=2)
+    lax.fori_loop(0, owners, one_owner, 0, unroll=owners)
     table = window_ref[...]
     date_ref[...] = dot(power_ref[...].reshape(16 * dates, 2 * LANES), table)
     sum_ref[...] = dot(split_ref[...].reshape(32 * pair_total, 2 * LANES), table)
@@ -355,8 +362,7 @@
 
 
 def filter_kernel(
-    ratio_ref, sample_high_ref, sample_low_ref, place_table_ref, line_high_ref, line_low_ref,
-    back_high_ref, back_low_ref, end_high_ref, end_low_ref,
+    ratio_ref, sample_ref, place_table_ref, line_ref, back_ref, end_ref,
     filtered_ref, coherence_ref, high_ref, low_ref, size_ref,
 ):
     pairs = coherence_ref.shape[0]
@@ -391,45 +397,44 @@
         lines = slice(pair * PATCH, (pair + 1) * PATCH)
         magnitude = dot_rows(place_table_ref[...], size_ref[lines])
         coherence_ref[pair] = magnitude.astype(coherence_ref.dtype)
-    spread = (
-        dot(high_ref[...], sample_high_ref[...])
-        + dot(low_ref[...], sample_high_ref[...])
-        + dot(high_ref[...], sample_low_ref[...])
-    )
+    spread = dot(
+        jnp.concatenate([high_ref[...], low_ref[...], high_ref[...]], 1), sample_ref[...]
+    )
+    left = lax.broadcasted_iota(jnp.int32, (HALF, LANES), 1) < PATCH
     columns = []
     for half in range(2):
-        for pair in range(pairs):
-            start = pair * PATCH + half * HALF
-            part = spread[start : start + HALF]
-            columns.append(jnp.concatenate([part[:, :LANES], part[:, LANES:]], 0))
-    high, low = rounded_parts(jnp.concatenate(columns, 1))
-    spectrum = (
-        dot(line_high_ref[...], high) + dot(line_high_ref[...], low) + dot(line_low_ref[...], high)
-    )
-    width = pairs * LANES
-    top = spectrum[:, :width]
-    bottom = spectrum[:, width:]
-    sign = 1.0 - 2.0 * (lax.broadcasted_iota(jnp.int32, (PATCH, width), 0) % 2).astype(jnp.float32)
+        first = spread[half * HALF : (half + 1) * HALF]
+        second = spread[PATCH + half * HALF : PATCH + (half + 1) * HALF]
+        real = jnp.where(left, first, pltpu.roll(second, PATCH, 1))
+        imag = jnp.where(left, pltpu.roll(first, PATCH, 1), second)
+        columns.append(jnp.concatenate([real, imag], 0))
+        columns.append(jnp.concatenate([imag, -real], 0))
+    spectrum = dot(line_ref[...], three_parts(jnp.concatenate(columns, 1), 0))
+    top_real, top_imag, low_real, low_imag = (
+        spectrum[:, index * LANES : (index + 1) * LANES] for index in range(4)
+    )
+    sign = 1.0 - 2.0 * (lax.broadcasted_iota(jnp.int32, (PATCH, LANES), 0) % 2).astype(jnp.float32)
+    side = lax.broadcasted_iota(jnp.int32, (1, LANES), 1) < PATCH
     weighted = []
-    for patch in (top, top + sign * bottom, bottom):
-        parts = []
-        for pair in range(pairs):
-            values = patch[:, pair * LANES : (pair + 1) * LANES]
-            square = values * values
-            energy = square + pltpu.roll(square, LANES // 2, 1)
-            weight = lax.rsqrt(lax.rsqrt(energy + 1.0))
-            total = jnp.sum(weight, axis=(0, 1), keepdims=True)
-            parts.append(values * weight * ((2.0 * PATCH * PATCH) / total))
-        weighted.append(jnp.concatenate(parts, 1))
-    weighted = [weighted[0], weighted[1], weighted[1], weighted[2]]
-    high, low = rounded_parts(jnp.concatenate(weighted, 0))
-    back = (
-        dot_rows(back_high_ref[...], high)
-        + dot_rows(back_high_ref[...], low)
-        + dot_rows(back_low_ref[...], high)
-    )
-    high, low = rounded_parts(jnp.concatenate([back[: width // 2], back[width // 2 :]], 1))
-    lines = dot(high, end_high_ref[...]) + dot(low, end_high_ref[...]) + dot(high, end_low_ref[...])
+    for real, imag in (
+        (top_real, top_imag),
+        (top_real + sign * low_real, top_imag + sign * low_imag),
+        (low_real, low_imag),
+    ):
+        weight = lax.rsqrt(lax.rsqrt(real * real + imag * imag + 1.0))
+        total = jnp.sum(weight, axis=0, keepdims=True)
+        first = jnp.sum(jnp.where(side, total, 0.0), axis=1, keepdims=True)
+        second = jnp.sum(jnp.where(side, 0.0, total), axis=1, keepdims=True)
+        weight = weight * ((1.0 * PATCH * PATCH) / jnp.where(side, first, second))
+        weighted.append(three_parts(jnp.concatenate([real * weight, imag * weight], 1), 1))
+    back = dot_rows(
+        back_ref[...],
+        jnp.concatenate([weighted[0], weighted[1], weighted[1], weighted[2]], 0),
+    )
+    count = back.shape[0] // 2
+    lines = dot(
+        three_parts(jnp.concatenate([back[:count], back[count:]], 1), 1), end_ref[...]
+    )
     filtered_ref[...] = lines.reshape(filtered_ref.shape).astype(filtered_ref.dtype)
 
 
@@ -455,16 +460,17 @@
     view = acquisitions.reshape(dates_here, line_count, 2, columns, LANES)
     view = view.transpose(0, 1, 3, 2, 4).reshape(dates_here, line_count * columns * 2, LANES)
 
-    def block(source, offset):
-        return lax.dynamic_slice_in_dim(source, (group ^ offset) * rows, rows, 1)
-
     step = across * cores
-    received = {offset: swap(block(view, offset), offset * step) for offset in (3, 1, 2)}
-    own = block(view, 0)
+    vmem = pl.BlockSpec(memory_space=pltpu.VMEM)
+    smem = pl.BlockSpec(memory_space=pltpu.SMEM)
+
+    def block(offset):
+        return lax.dynamic_slice_in_dim(view, (group ^ offset) * rows, rows, 1)
+
+    received = {offset: swap(block(offset), offset * step) for offset in (3, 1, 2)}
+    own = block(0)
     listed = jnp.broadcast_to(date_pairs.reshape(1, -1), (total, 2 * pairs_here))
     pair_list = lax.all_to_all(listed, names, 0, 0, tiled=True)
-    vmem = pl.BlockSpec(memory_space=pltpu.VMEM)
-    smem = pl.BlockSpec(memory_space=pltpu.SMEM)
     ratios = pl.pallas_call(
         products_kernel,
         name="products",
@@ -493,9 +499,13 @@
     arrived = lax.all_to_all(ratios, names, 0, 0, tiled=True)
     sample_table, place_table = sample_tables(cells, look_samples, across)
     line_table, end_table = line_tables()
-    tables = []
-    for table in (sample_table, None, line_table, back_table(pairs_here), end_table):
-        tables += [place_table] if table is None else list(split_table(table))
+    tables = [
+        split_table(sample_table, 0),
+        place_table,
+        split_table(line_table, 1),
+        split_table(back_table(pairs_here), 1),
+        split_table(end_table, 0),
+    ]
     filtered, coherence = pl.pallas_call(
         filter_kernel,
         name="filter",

time: 35.1 us -> 34.6 us (0.986)
  Pallas kernels: 3.9 us -> 3.51 us
where the time goes in v3:
time: 34.6 us; the launch traced here: 34.3 us
  blocking collectives  23 us (66%)
  starting transfers between devices  5.71 us (17%)
  Pallas kernels  3.51 us (10%)
  local copies, waits for them, and re-layouts  1.35 us (4%)
  between operations  0.75 us (2%)
    all_to_all x1, blocking collectives, fast_local(): pair_list = lax.all_to_all(listed, names, 0, 0, tiled=True)  12.7 us
    all_to_all x1, blocking collectives, fast_local(): arrived = lax.all_to_all(ratios, names, 0, 0, tiled=True)  10.3 us
    ppermute x3, starting transfers between devices, swap(): return lax.ppermute(values, names, [(i, i ^ offset) for i in range(total)])  5.71 us
    pallas_call x1, Pallas kernels, fast_local(): pl.pallas_call(filter_kernel, name='filter', out_shape=[jax.ShapeDtypeStr...  1.92 us
    pallas_call x1, Pallas kernels, fast_local(): pl.pallas_call(products_kernel, name='products', out_shape=jax.ShapeDtype...  1.59 us
    dynamic_slice x1, local copies, waits for them, and re-layouts, block(): return lax.dynamic_slice_in_dim(view, (group ^ offset) * rows, rows, 1)  1.22 us
  transfers between devices with their start and end apart: 3, of which 0 were waited for; matrix products, arithmetic and copies ran while one was open for 0% of the time, Pallas kernels for 0%

profile of v3, /device:TPU:0, one launch (start us, length us, event | category | flops | bytes accessed | tf_op | source)
XLA Modules:
  0.0 34.3 jit_solution(14505875667185128012)
XLA Ops:
  0.7 0.0 copy-start.6
  0.7 0.0 copy-start.3
  0.7 0.0 copy-start.1
  0.7 0.0 copy-start.2
  0.7 1.2 %constant_dynamic-slice_fusion = (bf16[4,128,128]{2,1,0:T(8,128)(2,1)S(1)}, bf16[4,128,128]{2,1,0:T(8,128)(2,1)S(1)}, bf16[4,128,128]{2,1,0:T(8,128)(2,1)S(1)}, bf16[4,128,128]{2,1,0:T(8,128)(2,1)S(1)}) fusion(bf16[4,512,128]{2,1,0:T(8,128)(2,1)} %bitcast.10, s32[]{:T(128)S(6)} %select_n.15, s32[]{:T(128)S(6)} %select_n.14, s32[]{:T(128)S(6)} %select_n.13, ...), kind=kLoop, calls=%fused_computation | loop fusion | bytes 1048592 | tf_op jit(solution)/shard_map/dynamic_slice | solution.py:468
  1.9 0.0 copy-start
  1.9 3.1 %collective-permute-start = (bf16[4,128,128]{2,1,0:T(8,128)(2,1)S(1)}, bf16[4,128,128]{2,1,0:T(8,128)(2,1)S(1)}, u32[]{:S(2)}, u32[]{:S(2)}) collective-permute-start(bf16[4,128,128]{2,1,0:T(8,128)(2,1)S(1)} %get-tuple-element.8), channel_id=1, source_target_pairs={{0,4},{1,5},{2,6},{3,7},{4,0},{5,1},{6,2},{7,3},{8,12},{9,13},{10,... | collective-permute-start | bytes 393224 | tf_op jit(solution)/shard_map/ppermute | solution.py:458
  5.0 2.6 %collective-permute-start.1 = (bf16[4,128,128]{2,1,0:T(8,128)(2,1)S(1)}, bf16[4,128,128]{2,1,0:T(8,128)(2,1)S(1)}, u32[]{:S(2)}, u32[]{:S(2)}) collective-permute-start(bf16[4,128,128]{2,1,0:T(8,128)(2,1)S(1)} %get-tuple-element.7), channel_id=1, source_target_pairs={{0,8},{1,9},{2,10},{3,11},{4,12},{5,13},{6,14},{7,15},{8,0},{9,1},... | collective-permute-start | bytes 393224 | tf_op jit(solution)/shard_map/ppermute | solution.py:458
  7.6 0.0 collective-permute-start.2
  7.6 0.0 copy-done.6
  7.6 0.1 broadcast_in_dim.7
  7.7 12.7 %all_to_all.13 = s32[16,1,4]{2,1,0:T(1,128)S(1)} all-to-all(s32[16,1,4]{2,1,0:T(1,128)S(1)} %broadcast_in_dim.8), channel_id=1, replica_groups=mesh['tile'=2,'date'=4,'rng'=2,'az'=2] {'date','rng','az'}, dimensions={0} | all-to-all | bytes 512 | tf_op jit(solution)/shard_map/all_to_all | solution.py:473
  20.4 0.0 collective-permute-done.near_ref
  20.4 0.0 collective-permute-done.1.far_ref
  20.5 0.0 collective-permute-done.2.last_ref
  20.5 0.0 copy-done.3
  20.5 1.6 %products.1 = f32[16,4,128]{2,1,0:T(4,128)S(1)} custom-call(s32[1]{0:T(128)} %bitcast.place_ref, s32[16,4]{1,0:T(8,128)S(1)} %bitcast.9, bf16[4,128,128]{2,1,0:T(8,128)(2,1)S(1)} %get-tuple-element.9.own_ref, bf16[4,128,128]{2,1,0:T(8,128)(2,1)S(1)} %collective-permute-done.near_ref, bf16[4,128,128]{2,1,0:T(8,128)(2,1)S(1)} %collective-permute-done.1.far_ref, ...), custom_call_target="tpu_custom_call" | custom-call | tf_op jit(solution)/shard_map/products/pallas_call | solution.py:474
  22.1 0.0 copy-start.4
  22.1 0.0 copy-start.5
  22.1 10.3 %all_to_all.14.ratio_ref = f32[16,4,128]{2,1,0:T(4,128)S(1)} all-to-all(f32[16,4,128]{2,1,0:T(4,128)S(1)} %products.1), channel_id=1, replica_groups=mesh['tile'=2,'date'=4,'rng'=2,'az'=2] {'date','rng','az'}, dimensions={0} | all-to-all | bytes 65536 | tf_op jit(solution)/shard_map/all_to_all | solution.py:499
  32.4 0.0 copy-done.1
  32.4 0.0 copy-done.2
  32.4 0.0 copy-done
  32.4 0.0 copy-done.4
  32.4 0.0 copy-done.5
  32.4 1.9 %filter.1 = (bf16[2,2,32,64]{3,2,1,0:T(8,128)(2,1)}, bf16[2,32,64]{2,1,0:T(8,128)(2,1)}) custom-call(f32[16,4,128]{2,1,0:T(4,128)S(1)} %all_to_all.14.ratio_ref, bf16[1536,128]{1,0:T(8,128)(2,1)S(1)} %copy-done, bf16[32,256]{1,0:T(8,128)(2,1)S(1)} %copy-done.5, bf16[64,192]{1,0:T(8,128)(2,1)S(1)} %copy-done.4, bf16[256,768]{1,0:T(8,128)(2,1)S(1)} %copy-done.1, ...), custom_call_target="tpu_custom_call" | custom-call | tf_op jit(solution)/shard_map/filter/pallas_call | solution.py:509
  (1 shorter events, 0.0 us)
Async XLA Ops:
  0.7 7.0 %copy-start.6 = (s32[2,2]{1,0:T(2,128)S(1)}, s32[2,2]{1,0:T(2,128)}, u32[]{:S(2)}) copy-start(s32[2,2]{1,0:T(2,128)} %param.9) | copy-start | bytes 52
  0.7 19.8 %copy-start.3 = (bf16[256,128]{1,0:T(8,128)(2,1)S(1)}, bf16[256,128]{1,0:T(8,128)(2,1)}, u32[]{:S(2)}) copy-start(bf16[256,128]{1,0:T(8,128)(2,1)} %constant.29.clone.window_ref) | copy-start | bytes 196612
  0.7 31.7 %copy-start.1 = (bf16[256,768]{1,0:T(8,128)(2,1)S(1)}, bf16[256,768]{1,0:T(8,128)(2,1)}, u32[]{:S(2)}) copy-start(bf16[256,768]{1,0:T(8,128)(2,1)} %constant.33.clone.back_ref) | copy-start | bytes 1179652
  0.7 31.7 %copy-start.2 = (bf16[1536,64]{1,0:T(8,128)(2,1)S(1)}, bf16[1536,64]{1,0:T(8,128)(2,1)}, u32[]{:S(2)}) copy-start(bf16[1536,64]{1,0:T(8,128)(2,1)} %constant.34.clone.end_ref) | copy-start | bytes 589828
  1.9 30.5 %copy-start = (bf16[1536,128]{1,0:T(8,128)(2,1)S(1)}, bf16[1536,128]{1,0:T(8,128)(2,1)}, u32[]{:S(2)}) copy-start(bf16[1536,128]{1,0:T(8,128)(2,1)} %constant.30.clone.sample_ref) | copy-start | bytes 1179652
  1.9 18.5 %collective-permute-start = (bf16[4,128,128]{2,1,0:T(8,128)(2,1)S(1)}, bf16[4,128,128]{2,1,0:T(8,128)(2,1)S(1)}, u32[]{:S(2)}, u32[]{:S(2)}) collective-permute-start(bf16[4,128,128]{2,1,0:T(8,128)(2,1)S(1)} %get-tuple-element.8), channel_id=1, source_target_pairs={{0,4},{1,5},{2,6},{3,7},{4,0},{5,1},{6,2},{7,3},{8,12},{9,13},{10,... | collective-permute-start | bytes 393224 | tf_op jit(solution)/shard_map/ppermute | solution.py:458
  5.0 15.4 %collective-permute-start.1 = (bf16[4,128,128]{2,1,0:T(8,128)(2,1)S(1)}, bf16[4,128,128]{2,1,0:T(8,128)(2,1)S(1)}, u32[]{:S(2)}, u32[]{:S(2)}) collective-permute-start(bf16[4,128,128]{2,1,0:T(8,128)(2,1)S(1)} %get-tuple-element.7), channel_id=1, source_target_pairs={{0,8},{1,9},{2,10},{3,11},{4,12},{5,13},{6,14},{7,15},{8,0},{9,1},... | collective-permute-start | bytes 393224 | tf_op jit(solution)/shard_map/ppermute | solution.py:458
  7.6 12.8 %collective-permute-start.2 = (bf16[4,128,128]{2,1,0:T(8,128)(2,1)S(1)}, bf16[4,128,128]{2,1,0:T(8,128)(2,1)S(1)}, u32[]{:S(2)}, u32[]{:S(2)}) collective-permute-start(bf16[4,128,128]{2,1,0:T(8,128)(2,1)S(1)} %get-tuple-element.6), channel_id=1, source_target_pairs={{0,12},{1,13},{2,14},{3,15},{4,8},{5,9},{6,10},{7,11},{8,4},{9,5},... | collective-permute-start | bytes 393224 | tf_op jit(solution)/shard_map/ppermute | solution.py:458
  22.1 10.3 %copy-start.4 = (bf16[64,192]{1,0:T(8,128)(2,1)S(1)}, bf16[64,192]{1,0:T(8,128)(2,1)}, u32[]{:S(2)}) copy-start(bf16[64,192]{1,0:T(8,128)(2,1)} %constant.32.clone.line_ref) | copy-start | bytes 73732
  22.1 10.3 %copy-start.5 = (bf16[32,256]{1,0:T(8,128)(2,1)S(1)}, bf16[32,256]{1,0:T(8,128)(2,1)}, u32[]{:S(2)}) copy-start(bf16[32,256]{1,0:T(8,128)(2,1)} %constant.31.clone.place_table_ref) | copy-start | bytes 49156

commit v4 on v3

--- a/solution.py
+++ b/solution.py
@@ -236,6 +236,7 @@
         return np.concatenate([top, bottom], 1)
 
     end = np.concatenate([back(cosine), back(sine)], 0) / PATCH**2
+    end = np.concatenate([end, np.zeros((end.shape[0], 2 * LANES - PATCH))], 1)
     return (np.concatenate([cosine, sine], 1), end)
 
 
@@ -262,30 +263,33 @@
     )
 
 
-def products_kernel(
-    place_ref, pair_ref, own_ref, near_ref, far_ref, last_ref, window_ref,
-    out_ref,
-    part_ref, split_ref, power_ref, sum_ref, date_ref, root_ref, scale_ref,
+def total(terms):
+    while len(terms) > 1:
+        terms = [a + b for a, b in zip(terms[::2], terms[1::2])]
+    return terms[0]
+
+
+def fold(ref, count):
+    lane = lax.broadcasted_iota(jnp.int32, (count, LANES), 1)
+    look = lane // 16
+    source = look % 2 * 8 + look // 4 * 4 + lane // 8 % 2 * 2 + look // 2 % 2
+    out = ref[pl.ds(0, count, stride=16), :]
+    for pick in range(1, 16):
+        out = jnp.where(source == pick, ref[pl.ds(pick, count, stride=16), :], out)
+    return out * (1.0 / (LOOK_AZ * LOOK_RG))
+
+
+def unpack_kernel(
+    place_ref, own_ref, near_ref, far_ref, last_ref, window_ref,
+    part_ref, root_ref,
+    power_ref, date_ref,
 ):
     group = place_ref[0]
     dates_here = own_ref.shape[0]
     dates = part_ref.shape[0]
-    owners = pair_ref.shape[0]
-    pairs_here = pair_ref.shape[1] // 2
-    pair_total = owners * pairs_here
     row = lax.broadcasted_iota(jnp.int32, (8, LANES), 0)
     low = row < 4
     even = row % 2 == 0
-
-    def split(target, slot, first, second):
-        high, rest = rounded_parts(jnp.concatenate([first, second], axis=0))
-        target[slot, :, :LANES] = high
-        target[slot, :, LANES:] = rest
-
-    def total(terms):
-        while len(terms) > 1:
-            terms = [a + b for a, b in zip(terms[::2], terms[1::2])]
-        return terms[0]
 
     for offset, ref in enumerate((own_ref, near_ref, far_ref, last_ref)):
         base = (group ^ offset) * dates_here
@@ -314,6 +318,24 @@
                 power_ref[base + index, 8 * pick : 8 * pick + 8, :LANES] = high
                 power_ref[base + index, 8 * pick : 8 * pick + 8, LANES:] = rest
 
+    date_ref[...] = dot(power_ref[...].reshape(16 * dates, 2 * LANES), window_ref[...])
+    root_ref[...] = lax.rsqrt(fold(date_ref, dates) + EPSILON)
+
+
+def products_kernel(
+    pair_ref, part_ref, root_ref, window_ref,
+    out_ref,
+    split_ref, sum_ref, scale_ref,
+):
+    owners = pair_ref.shape[0]
+    pairs_here = pair_ref.shape[1] // 2
+    pair_total = owners * pairs_here
+
+    def split(target, slot, first, second):
+        high, rest = rounded_parts(jnp.concatenate([first, second], axis=0))
+        target[slot, :, :LANES] = high
+        target[slot, :, LANES:] = rest
+
     def one_owner(owner, carry):
         for index in range(pairs_here):
             earlier = pair_ref[owner, index]
@@ -336,21 +358,7 @@
         return carry
 
     lax.fori_loop(0, owners, one_owner, 0, unroll=owners)
-    table = window_ref[...]
-    date_ref[...] = dot(power_ref[...].reshape(16 * dates, 2 * LANES), table)
-    sum_ref[...] = dot(split_ref[...].reshape(32 * pair_total, 2 * LANES), table)
-    share = 1.0 / (LOOK_AZ * LOOK_RG)
-
-    def fold(ref, count):
-        lane = lax.broadcasted_iota(jnp.int32, (count, LANES), 1)
-        look = lane // 16
-        source = look % 2 * 8 + look // 4 * 4 + lane // 8 % 2 * 2 + look // 2 % 2
-        out = ref[pl.ds(0, count, stride=16), :]
-        for pick in range(1, 16):
-            out = jnp.where(source == pick, ref[pl.ds(pick, count, stride=16), :], out)
-        return out * share
-
-    root_ref[...] = lax.rsqrt(fold(date_ref, dates) + EPSILON)
+    sum_ref[...] = dot(split_ref[...].reshape(32 * pair_total, 2 * LANES), window_ref[...])
     for owner in range(owners):
         for index in range(pairs_here):
             earlier = root_ref[pl.ds(pair_ref[owner, index], 1), :]
@@ -435,7 +443,7 @@
     lines = dot(
         three_parts(jnp.concatenate([back[:count], back[count:]], 1), 1), end_ref[...]
     )
-    filtered_ref[...] = lines.reshape(filtered_ref.shape).astype(filtered_ref.dtype)
+    filtered_ref[...] = lines[:, :PATCH].reshape(filtered_ref.shape).astype(filtered_ref.dtype)
 
 
 def fast_local(acquisitions, date_pairs, sizes):
@@ -471,31 +479,35 @@
     own = block(0)
     listed = jnp.broadcast_to(date_pairs.reshape(1, -1), (total, 2 * pairs_here))
     pair_list = lax.all_to_all(listed, names, 0, 0, tiled=True)
+    window = jnp.asarray(window_table(cells))
+    parts, roots = pl.pallas_call(
+        unpack_kernel,
+        name="unpack",
+        out_shape=[
+            jax.ShapeDtypeStruct((dates, 2, 2, LOOK_AZ, 8, LANES), jnp.float32),
+            jax.ShapeDtypeStruct((dates, cells), jnp.float32),
+        ],
+        in_specs=[smem] + [vmem] * 5,
+        out_specs=[vmem] * 2,
+        scratch_shapes=[
+            pltpu.VMEM((dates, 16, 2 * LANES), jnp.bfloat16),
+            pltpu.VMEM((16 * dates, cells), jnp.float32),
+        ],
+        compiler_params=pltpu.CompilerParams(vmem_limit_bytes=8 << 20),
+    )(group.reshape(1), own, received[1], received[2], received[3], window)
     ratios = pl.pallas_call(
         products_kernel,
         name="products",
         out_shape=jax.ShapeDtypeStruct((total, 2 * pairs_here, cells), jnp.float32),
-        in_specs=[smem, smem] + [vmem] * 5,
+        in_specs=[smem] + [vmem] * 3,
         out_specs=vmem,
         scratch_shapes=[
-            pltpu.VMEM((dates, 2, 2, LOOK_AZ, 8, LANES), jnp.float32),
             pltpu.VMEM((2 * pair_total, 16, 2 * LANES), jnp.bfloat16),
-            pltpu.VMEM((dates, 16, 2 * LANES), jnp.bfloat16),
             pltpu.VMEM((32 * pair_total, cells), jnp.float32),
-            pltpu.VMEM((16 * dates, cells), jnp.float32),
-            pltpu.VMEM((dates, cells), jnp.float32),
             pltpu.VMEM((2 * pair_total, cells), jnp.float32),
         ],
-        compiler_params=pltpu.CompilerParams(vmem_limit_bytes=12 << 20),
-    )(
-        group.reshape(1),
-        pair_list,
-        own,
-        received[1],
-        received[2],
-        received[3],
-        jnp.asarray(window_table(cells)),
-    )
+        compiler_params=pltpu.CompilerParams(vmem_limit_bytes=8 << 20),
+    )(pair_list, parts, roots, window)
     arrived = lax.all_to_all(ratios, names, 0, 0, tiled=True)
     sample_table, place_table = sample_tables(cells, look_samples, across)
     line_table, end_table = line_tables()

time: 34.6 us -> 34.1 us (0.986)
  blocking collectives: 23 us -> 9.91 us
  starting transfers between devices: 5.71 us -> 11.8 us
  waiting for transfers between devices: 0.01 us -> 5.88 us
  local copies, waits for them, and re-layouts: 1.35 us -> 1.9 us
    all_to_all x1 -> x0, blocking collectives: 12.7 us -> none  [fast_local(): pair_list = lax.all_to_all(listed, names, 0, 0, tiled=True)]
    all_to_all x0 -> x1, starting transfers between devices: none -> 6.13 us  [fast_local(): pair_list = lax.all_to_all(listed, names, 0, 0, tiled=True)]
    ppermute x3, waiting for transfers between devices: 0.01 us -> 3.46 us  [swap(): return lax.ppermute(values, names, [(i, i ^ offset) for i in range(total)])]
    all_to_all x0 -> x1, waiting for transfers between devices: none -> 2.42 us  [fast_local(): pair_list = lax.all_to_all(listed, names, 0, 0, tiled=True)]
    broadcast_in_dim x2, local copies, waits for them, and re-layouts: 0.09 us -> 0.69 us  [fast_local(): jnp.broadcast_to(date_pairs.reshape(1, -1), (total, 2 * pairs_here))]
    pallas_call x0 -> x1, Pallas kernels: none -> 0.46 us  [fast_local(): pl.pallas_call(unpack_kernel, name='unpack', out_shape=[jax.ShapeDtypeStr...]
    all_to_all x1, blocking collectives: 10.3 us -> 9.91 us  [fast_local(): arrived = lax.all_to_all(ratios, names, 0, 0, tiled=True)]
    pallas_call x1, Pallas kernels: 1.59 us -> 1.23 us  [fast_local(): pl.pallas_call(products_kernel, name='products', out_shape=jax.ShapeDtype...]
  transfers between devices with their start and end apart: 3 -> 4, of which waited for: 0 -> 2; matrix products, arithmetic and copies ran while one was open for 0% -> 2% of each run, Pallas kernels for 0% -> 1%
where the time goes in v4:
time: 34.1 us; the launch traced here: 33.9 us
  starting transfers between devices  11.8 us (35%)
  blocking collectives  9.91 us (29%)
  waiting for transfers between devices  5.88 us (17%)
  Pallas kernels  3.61 us (11%)
  local copies, waits for them, and re-layouts  1.9 us (6%)
  between operations  0.74 us (2%)
    all_to_all x1, blocking collectives, fast_local(): arrived = lax.all_to_all(ratios, names, 0, 0, tiled=True)  9.91 us
    all_to_all x1, starting transfers between devices, fast_local(): pair_list = lax.all_to_all(listed, names, 0, 0, tiled=True)  6.13 us
    ppermute x3, starting transfers between devices, swap(): return lax.ppermute(values, names, [(i, i ^ offset) for i in range(total)])  5.71 us
    ppermute x3, waiting for transfers between devices, swap(): return lax.ppermute(values, names, [(i, i ^ offset) for i in range(total)])  3.46 us
    all_to_all x1, waiting for transfers between devices, fast_local(): pair_list = lax.all_to_all(listed, names, 0, 0, tiled=True)  2.42 us
    pallas_call x1, Pallas kernels, fast_local(): pl.pallas_call(filter_kernel, name='filter', out_shape=[jax.ShapeDtypeStr...  1.92 us
    pallas_call x1, Pallas kernels, fast_local(): pl.pallas_call(products_kernel, name='products', out_shape=jax.ShapeDtype...  1.23 us
    dynamic_slice x1, local copies, waits for them, and re-layouts, block(): return lax.dynamic_slice_in_dim(view, (group ^ offset) * rows, rows, 1)  1.17 us
  transfers between devices with their start and end apart: 4, of which 2 were waited for; matrix products, arithmetic and copies ran while one was open for 2% of the time, Pallas kernels for 1%

profile of v4, /device:TPU:0, one launch (start us, length us, event | category | flops | bytes accessed | tf_op | source)
XLA Modules:
  0.0 33.9 jit_solution(3820349182334995025)
XLA Ops:
  0.7 0.0 copy-start.3
  0.7 1.2 %constant_dynamic-slice_fusion = (bf16[4,128,128]{2,1,0:T(8,128)(2,1)S(1)}, bf16[4,128,128]{2,1,0:T(8,128)(2,1)S(1)}, bf16[4,128,128]{2,1,0:T(8,128)(2,1)S(1)}, bf16[4,128,128]{2,1,0:T(8,128)(2,1)S(1)}) fusion(bf16[4,512,128]{2,1,0:T(8,128)(2,1)} %bitcast.10, s32[]{:T(128)S(6)} %select_n.15, s32[]{:T(128)S(6)} %select_n.14, s32[]{:T(128)S(6)} %select_n.13, ...), kind=kLoop, calls=%fused_computation | loop fusion | bytes 1048592 | tf_op jit(solution)/shard_map/dynamic_slice | solution.py:476
  1.8 3.1 %collective-permute-start = (bf16[4,128,128]{2,1,0:T(8,128)(2,1)S(1)}, bf16[4,128,128]{2,1,0:T(8,128)(2,1)S(1)}, u32[]{:S(2)}, u32[]{:S(2)}) collective-permute-start(bf16[4,128,128]{2,1,0:T(8,128)(2,1)S(1)} %get-tuple-element.12), channel_id=1, source_target_pairs={{0,4},{1,5},{2,6},{3,7},{4,0},{5,1},{6,2},{7,3},{8,12},{9,13},{10,... | collective-permute-start | bytes 393224 | tf_op jit(solution)/shard_map/ppermute | solution.py:466
  5.0 0.0 copy-start.6
  5.0 2.6 %collective-permute-start.1 = (bf16[4,128,128]{2,1,0:T(8,128)(2,1)S(1)}, bf16[4,128,128]{2,1,0:T(8,128)(2,1)S(1)}, u32[]{:S(2)}, u32[]{:S(2)}) collective-permute-start(bf16[4,128,128]{2,1,0:T(8,128)(2,1)S(1)} %get-tuple-element.11), channel_id=1, source_target_pairs={{0,8},{1,9},{2,10},{3,11},{4,12},{5,13},{6,14},{7,15},{8,0},{9,1},... | collective-permute-start | bytes 393224 | tf_op jit(solution)/shard_map/ppermute | solution.py:466
  7.6 0.0 collective-permute-start.2
  7.6 0.0 copy-done.6
  7.6 0.1 broadcast_in_dim.7
  7.6 0.6 %broadcast_in_dim.8 = s32[16,1,4]{2,1,0:T(1,128)} broadcast(s32[4]{0:T(128)S(1)} %broadcast_in_dim.7), dimensions={2} | broadcast | bytes 272 | tf_op jit(solution)/shard_map/broadcast_in_dim | solution.py:480
  8.2 6.1 %all-to-all-start = ((s32[16,1,4]{2,1,0:T(1,128)}), s32[16,1,4]{2,1,0:T(1,128)S(1)}, u32[]{:S(2)}, u32[]{:S(2)}) async-start(s32[16,1,4]{2,1,0:T(1,128)} %broadcast_in_dim.8), calls=%async_computation | async-start | bytes 16384 | tf_op jit(solution)/shard_map/all_to_all | solution.py:481
  14.4 0.0 collective-permute-done.near_ref
  14.4 3.5 %collective-permute-done.1.far_ref = bf16[4,128,128]{2,1,0:T(8,128)(2,1)S(1)} collective-permute-done((bf16[4,128,128]{2,1,0:T(8,128)(2,1)S(1)}, bf16[4,128,128]{2,1,0:T(8,128)(2,1)S(1)}, u32[]{:S(2)}, u32[]{:S(2)}) %collective-permute-start.1) | collective-permute-done | bytes 131104 | tf_op jit(solution)/shard_map/ppermute | solution.py:466
  17.8 0.0 collective-permute-done.2.last_ref
  17.9 0.0 copy-done.3
  17.9 0.0 copy-start
  17.9 0.5 %unpack.1 = (f32[16,2,2,4,8,128]{5,4,3,2,1,0:T(8,128)S(1)}, f32[16,128]{1,0:T(8,128)S(1)}) custom-call(s32[1]{0:T(128)} %bitcast.1.place_ref, bf16[4,128,128]{2,1,0:T(8,128)(2,1)S(1)} %get-tuple-element.13.own_ref, bf16[4,128,128]{2,1,0:T(8,128)(2,1)S(1)} %collective-permute-done.near_ref, bf16[4,128,128]{2,1,0:T(8,128)(2,1)S(1)} %collective-permute-done.1.far_ref, ...), custom_call_target="tpu_custom_call" | custom-call | tf_op jit(solution)/shard_map/unpack/pallas_call | solution.py:483
  18.3 2.4 %all-to-all-done = s32[16,1,4]{2,1,0:T(1,128)S(1)} async-done(((s32[16,1,4]{2,1,0:T(1,128)}), s32[16,1,4]{2,1,0:T(1,128)S(1)}, u32[]{:S(2)}, u32[]{:S(2)}) %all-to-all-start) | async-done | bytes 288 | tf_op jit(solution)/shard_map/all_to_all | solution.py:481
  20.7 0.0 copy-start.1
  20.7 0.0 copy-start.2
  20.7 1.2 %products.1 = f32[16,4,128]{2,1,0:T(4,128)S(1)} custom-call(s32[16,4]{1,0:T(8,128)S(1)} %bitcast.9, f32[16,2,2,4,8,128]{5,4,3,2,1,0:T(8,128)S(1)} %get-tuple-element.6.part_ref, f32[16,128]{1,0:T(8,128)S(1)} %get-tuple-element.7.root_ref, bf16[256,128]{1,0:T(8,128)(2,1)S(1)} %copy-done.3), custom_call_target="tpu_custom_call" | custom-call | tf_op jit(solution)/shard_map/products/pallas_call | solution.py:498
  22.0 0.0 copy-start.4
  22.0 0.0 copy-start.5
  22.0 9.9 %all_to_all.13.ratio_ref = f32[16,4,128]{2,1,0:T(4,128)S(1)} all-to-all(f32[16,4,128]{2,1,0:T(4,128)S(1)} %products.1), channel_id=1, replica_groups=mesh['tile'=2,'date'=4,'rng'=2,'az'=2] {'date','rng','az'}, dimensions={0} | all-to-all | bytes 65536 | tf_op jit(solution)/shard_map/all_to_all | solution.py:511
  31.9 0.0 copy-done
  31.9 0.0 copy-done.1
  31.9 0.0 copy-done.2
  31.9 0.0 copy-done.4
  31.9 0.0 copy-done.5
  32.0 1.9 %filter.1 = (bf16[2,2,32,64]{3,2,1,0:T(8,128)(2,1)}, bf16[2,32,64]{2,1,0:T(8,128)(2,1)}) custom-call(f32[16,4,128]{2,1,0:T(4,128)S(1)} %all_to_all.13.ratio_ref, bf16[1536,128]{1,0:T(8,128)(2,1)S(1)} %copy-done.1, bf16[32,256]{1,0:T(8,128)(2,1)S(1)} %copy-done.5, bf16[64,192]{1,0:T(8,128)(2,1)S(1)} %copy-done.4, bf16[256,768]{1,0:T(8,128)(2,1)S(1)} %copy-done.2, ...), custom_call_target="tpu_custom_call" | custom-call | tf_op jit(solution)/shard_map/filter/pallas_call | solution.py:521
Async XLA Ops:
  0.7 17.2 %copy-start.3 = (bf16[256,128]{1,0:T(8,128)(2,1)S(1)}, bf16[256,128]{1,0:T(8,128)(2,1)}, u32[]{:S(2)}) copy-start(bf16[256,128]{1,0:T(8,128)(2,1)} %constant.29.clone.window_ref) | copy-start | bytes 196612
  1.8 12.5 %collective-permute-start = (bf16[4,128,128]{2,1,0:T(8,128)(2,1)S(1)}, bf16[4,128,128]{2,1,0:T(8,128)(2,1)S(1)}, u32[]{:S(2)}, u32[]{:S(2)}) collective-permute-start(bf16[4,128,128]{2,1,0:T(8,128)(2,1)S(1)} %get-tuple-element.12), channel_id=1, source_target_pairs={{0,4},{1,5},{2,6},{3,7},{4,0},{5,1},{6,2},{7,3},{8,12},{9,13},{10,... | collective-permute-start | bytes 393224 | tf_op jit(solution)/shard_map/ppermute | solution.py:466
  5.0 2.6 %copy-start.6 = (s32[2,2]{1,0:T(2,128)S(1)}, s32[2,2]{1,0:T(2,128)}, u32[]{:S(2)}) copy-start(s32[2,2]{1,0:T(2,128)} %param.9) | copy-start | bytes 52
  5.0 12.9 %collective-permute-start.1 = (bf16[4,128,128]{2,1,0:T(8,128)(2,1)S(1)}, bf16[4,128,128]{2,1,0:T(8,128)(2,1)S(1)}, u32[]{:S(2)}, u32[]{:S(2)}) collective-permute-start(bf16[4,128,128]{2,1,0:T(8,128)(2,1)S(1)} %get-tuple-element.11), channel_id=1, source_target_pairs={{0,8},{1,9},{2,10},{3,11},{4,12},{5,13},{6,14},{7,15},{8,0},{9,1},... | collective-permute-start | bytes 393224 | tf_op jit(solution)/shard_map/ppermute | solution.py:466
  7.6 10.3 %collective-permute-start.2 = (bf16[4,128,128]{2,1,0:T(8,128)(2,1)S(1)}, bf16[4,128,128]{2,1,0:T(8,128)(2,1)S(1)}, u32[]{:S(2)}, u32[]{:S(2)}) collective-permute-start(bf16[4,128,128]{2,1,0:T(8,128)(2,1)S(1)} %get-tuple-element.10), channel_id=1, source_target_pairs={{0,12},{1,13},{2,14},{3,15},{4,8},{5,9},{6,10},{7,11},{8,4},{9,5},... | collective-permute-start | bytes 393224 | tf_op jit(solution)/shard_map/ppermute | solution.py:466
  8.2 12.5 %all-to-all-start = ((s32[16,1,4]{2,1,0:T(1,128)}), s32[16,1,4]{2,1,0:T(1,128)S(1)}, u32[]{:S(2)}, u32[]{:S(2)}) async-start(s32[16,1,4]{2,1,0:T(1,128)} %broadcast_in_dim.8), calls=%async_computation | async-start | bytes 16384 | tf_op jit(solution)/shard_map/all_to_all | solution.py:481
  17.9 14.1 %copy-start = (bf16[1536,256]{1,0:T(8,128)(2,1)S(1)}, bf16[1536,256]{1,0:T(8,128)(2,1)}, u32[]{:S(2)}) copy-start(bf16[1536,256]{1,0:T(8,128)(2,1)} %constant.34.clone.end_ref) | copy-start | bytes 2359300
  20.7 11.2 %copy-start.1 = (bf16[1536,128]{1,0:T(8,128)(2,1)S(1)}, bf16[1536,128]{1,0:T(8,128)(2,1)}, u32[]{:S(2)}) copy-start(bf16[1536,128]{1,0:T(8,128)(2,1)} %constant.30.clone.sample_ref) | copy-start | bytes 1179652
  20.7 11.2 %copy-start.2 = (bf16[256,768]{1,0:T(8,128)(2,1)S(1)}, bf16[256,768]{1,0:T(8,128)(2,1)}, u32[]{:S(2)}) copy-start(bf16[256,768]{1,0:T(8,128)(2,1)} %constant.33.clone.back_ref) | copy-start | bytes 1179652
  22.0 10.0 %copy-start.4 = (bf16[64,192]{1,0:T(8,128)(2,1)S(1)}, bf16[64,192]{1,0:T(8,128)(2,1)}, u32[]{:S(2)}) copy-start(bf16[64,192]{1,0:T(8,128)(2,1)} %constant.32.clone.line_ref) | copy-start | bytes 73732
  22.0 9.9 %copy-start.5 = (bf16[32,256]{1,0:T(8,128)(2,1)S(1)}, bf16[32,256]{1,0:T(8,128)(2,1)}, u32[]{:S(2)}) copy-start(bf16[32,256]{1,0:T(8,128)(2,1)} %constant.31.clone.place_table_ref) | copy-start | bytes 49156

commit v5 on v4

--- a/solution.py
+++ b/solution.py
@@ -14,6 +14,7 @@
 LOOK_RG = 16
 HALF = 32
 LANES = 128
+SHIFTS = (1, 2, 3)
 
 
 EPSILON = 1e-06
@@ -280,19 +281,20 @@
 
 
 def unpack_kernel(
-    place_ref, own_ref, near_ref, far_ref, last_ref, window_ref,
+    place_ref, own_ref, first_ref, second_ref, third_ref, window_ref,
     part_ref, root_ref,
     power_ref, date_ref,
 ):
     group = place_ref[0]
     dates_here = own_ref.shape[0]
     dates = part_ref.shape[0]
+    depth = dates // dates_here
     row = lax.broadcasted_iota(jnp.int32, (8, LANES), 0)
     low = row < 4
     even = row % 2 == 0
 
-    for offset, ref in enumerate((own_ref, near_ref, far_ref, last_ref)):
-        base = (group ^ offset) * dates_here
+    for shift, ref in zip((0, *SHIFTS), (own_ref, first_ref, second_ref, third_ref)):
+        base = lax.rem(group + depth - shift, depth) * dates_here
         for index in range(dates_here):
             values = ref[index].astype(jnp.float32).reshape(8, 2, 8, LANES)
             for pick in range(2):
@@ -462,9 +464,6 @@
     group = lax.axis_index("date")
     names = ("date", "rng", "az")
 
-    def swap(values, offset):
-        return lax.ppermute(values, names, [(i, i ^ offset) for i in range(total)])
-
     view = acquisitions.reshape(dates_here, line_count, 2, columns, LANES)
     view = view.transpose(0, 1, 3, 2, 4).reshape(dates_here, line_count * columns * 2, LANES)
 
@@ -472,10 +471,16 @@
     vmem = pl.BlockSpec(memory_space=pltpu.VMEM)
     smem = pl.BlockSpec(memory_space=pltpu.SMEM)
 
-    def block(offset):
-        return lax.dynamic_slice_in_dim(view, (group ^ offset) * rows, rows, 1)
-
-    received = {offset: swap(block(offset), offset * step) for offset in (3, 1, 2)}
+    def block(shift):
+        return lax.dynamic_slice_in_dim(view, lax.rem(group + shift, depth) * rows, rows, 1)
+
+    received = []
+    for shift in SHIFTS:
+        received.append(
+            lax.ppermute(
+                block(shift), names, [(i, (i + shift * step) % total) for i in range(total)]
+            )
+        )
     own = block(0)
     listed = jnp.broadcast_to(date_pairs.reshape(1, -1), (total, 2 * pairs_here))
     pair_list = lax.all_to_all(listed, names, 0, 0, tiled=True)
@@ -494,7 +499,7 @@
             pltpu.VMEM((16 * dates, cells), jnp.float32),
         ],
         compiler_params=pltpu.CompilerParams(vmem_limit_bytes=8 << 20),
-    )(group.reshape(1), own, received[1], received[2], received[3], window)
+    )(group.reshape(1), own, *received, window)
     ratios = pl.pallas_call(
         products_kernel,
         name="products",

time: 34.1 us -> 33.4 us (0.979)
  starting transfers between devices: 11.8 us -> 10.5 us
  waiting for transfers between devices: 5.88 us -> 6.44 us
    all_to_all x1, starting transfers between devices: 6.13 us -> 3.47 us  [fast_local(): pair_list = lax.all_to_all(listed, names, 0, 0, tiled=True)]
    ppermute x3, starting transfers between devices: 5.71 us -> 7.04 us  [fast_local(): lax.ppermute(block(shift), names, [(i, (i + shift * step) % total) for i...]
    all_to_all x1, waiting for transfers between devices: 2.42 us -> 3.32 us  [fast_local(): pair_list = lax.all_to_all(listed, names, 0, 0, tiled=True)]
    ppermute x3, waiting for transfers between devices: 3.46 us -> 3.12 us  [fast_local(): lax.ppermute(block(shift), names, [(i, (i + shift * step) % total) for i...]
where the time goes in v5:
time: 33.4 us; the launch traced here: 33.1 us
  starting transfers between devices  10.5 us (31%)
  blocking collectives  9.93 us (30%)
  waiting for transfers between devices  6.44 us (19%)
  Pallas kernels  3.6 us (11%)
  local copies, waits for them, and re-layouts  1.9 us (6%)
  between operations  0.75 us (2%)
    all_to_all x1, blocking collectives, fast_local(): arrived = lax.all_to_all(ratios, names, 0, 0, tiled=True)  9.93 us
    ppermute x3, starting transfers between devices, fast_local(): lax.ppermute(block(shift), names, [(i, (i + shift * step) % total) for i...  7.04 us
    all_to_all x1, starting transfers between devices, fast_local(): pair_list = lax.all_to_all(listed, names, 0, 0, tiled=True)  3.47 us
    all_to_all x1, waiting for transfers between devices, fast_local(): pair_list = lax.all_to_all(listed, names, 0, 0, tiled=True)  3.32 us
    ppermute x3, waiting for transfers between devices, fast_local(): lax.ppermute(block(shift), names, [(i, (i + shift * step) % total) for i...  3.12 us
    pallas_call x1, Pallas kernels, fast_local(): pl.pallas_call(filter_kernel, name='filter', out_shape=[jax.ShapeDtypeStr...  1.93 us
    pallas_call x1, Pallas kernels, fast_local(): pl.pallas_call(products_kernel, name='products', out_shape=jax.ShapeDtype...  1.23 us
    dynamic_slice x1, local copies, waits for them, and re-layouts, block(): lax.dynamic_slice_in_dim(view, lax.rem(group + shift, depth) * rows, rows...  1.17 us
  transfers between devices with their start and end apart: 4, of which 2 were waited for; matrix products, arithmetic and copies ran while one was open for 2% of the time, Pallas kernels for 1%

profile of v5, /device:TPU:0, one launch (start us, length us, event | category | flops | bytes accessed | tf_op | source)
XLA Modules:
  0.0 33.1 jit_solution(11319498322697522902)
XLA Ops:
  0.7 0.0 copy-start.3
  0.7 1.2 %constant_dynamic-slice_fusion = (bf16[4,128,128]{2,1,0:T(8,128)(2,1)S(1)}, bf16[4,128,128]{2,1,0:T(8,128)(2,1)S(1)}, bf16[4,128,128]{2,1,0:T(8,128)(2,1)S(1)}, bf16[4,128,128]{2,1,0:T(8,128)(2,1)S(1)}) fusion(bf16[4,512,128]{2,1,0:T(8,128)(2,1)} %bitcast.10, s32[]{:T(128)S(6)} %select_n.15, s32[]{:T(128)S(6)} %select_n.14, s32[]{:T(128)S(6)} %select_n.13, ...), kind=kLoop, calls=%fused_computation | loop fusion | bytes 1048592 | tf_op jit(solution)/shard_map/dynamic_slice | solution.py:475
  1.8 3.1 %collective-permute-start = (bf16[4,128,128]{2,1,0:T(8,128)(2,1)S(1)}, bf16[4,128,128]{2,1,0:T(8,128)(2,1)S(1)}, u32[]{:S(2)}, u32[]{:S(2)}) collective-permute-start(bf16[4,128,128]{2,1,0:T(8,128)(2,1)S(1)} %get-tuple-element.12), channel_id=1, source_target_pairs={{0,4},{1,5},{2,6},{3,7},{4,8},{5,9},{6,10},{7,11},{8,12},{9,13},{1... | collective-permute-start | bytes 393224 | tf_op jit(solution)/shard_map/ppermute | solution.py:480
  5.0 0.0 copy-start.6
  5.0 2.6 %collective-permute-start.1 = (bf16[4,128,128]{2,1,0:T(8,128)(2,1)S(1)}, bf16[4,128,128]{2,1,0:T(8,128)(2,1)S(1)}, u32[]{:S(2)}, u32[]{:S(2)}) collective-permute-start(bf16[4,128,128]{2,1,0:T(8,128)(2,1)S(1)} %get-tuple-element.11), channel_id=1, source_target_pairs={{0,8},{1,9},{2,10},{3,11},{4,12},{5,13},{6,14},{7,15},{8,0},{9,1},... | collective-permute-start | bytes 393224 | tf_op jit(solution)/shard_map/ppermute | solution.py:480
  7.5 1.3 %collective-permute-start.2 = (bf16[4,128,128]{2,1,0:T(8,128)(2,1)S(1)}, bf16[4,128,128]{2,1,0:T(8,128)(2,1)S(1)}, u32[]{:S(2)}, u32[]{:S(2)}) collective-permute-start(bf16[4,128,128]{2,1,0:T(8,128)(2,1)S(1)} %get-tuple-element.10), channel_id=1, source_target_pairs={{0,12},{1,13},{2,14},{3,15},{4,0},{5,1},{6,2},{7,3},{8,4},{9,5},{1... | collective-permute-start | bytes 393224 | tf_op jit(solution)/shard_map/ppermute | solution.py:480
  8.9 0.0 copy-done.6
  8.9 0.1 broadcast_in_dim.7
  9.0 0.6 %broadcast_in_dim.8 = s32[16,1,4]{2,1,0:T(1,128)} broadcast(s32[4]{0:T(128)S(1)} %broadcast_in_dim.7), dimensions={2} | broadcast | bytes 272 | tf_op jit(solution)/shard_map/broadcast_in_dim | solution.py:485
  9.6 3.5 %all-to-all-start = ((s32[16,1,4]{2,1,0:T(1,128)}), s32[16,1,4]{2,1,0:T(1,128)S(1)}, u32[]{:S(2)}, u32[]{:S(2)}) async-start(s32[16,1,4]{2,1,0:T(1,128)} %broadcast_in_dim.8), calls=%async_computation | async-start | bytes 16384 | tf_op jit(solution)/shard_map/all_to_all | solution.py:486
  13.1 0.0 collective-permute-done.first_ref
  13.1 3.1 %collective-permute-done.1.second_ref = bf16[4,128,128]{2,1,0:T(8,128)(2,1)S(1)} collective-permute-done((bf16[4,128,128]{2,1,0:T(8,128)(2,1)S(1)}, bf16[4,128,128]{2,1,0:T(8,128)(2,1)S(1)}, u32[]{:S(2)}, u32[]{:S(2)}) %collective-permute-start.1) | collective-permute-done | bytes 131104 | tf_op jit(solution)/shard_map/ppermute | solution.py:480
  16.2 0.0 collective-permute-done.2.third_ref
  16.2 0.0 copy-done.3
  16.2 0.0 copy-start
  16.2 0.4 %unpack.1 = (f32[16,2,2,4,8,128]{5,4,3,2,1,0:T(8,128)S(1)}, f32[16,128]{1,0:T(8,128)S(1)}) custom-call(s32[1]{0:T(128)} %bitcast.1.place_ref, bf16[4,128,128]{2,1,0:T(8,128)(2,1)S(1)} %get-tuple-element.13.own_ref, bf16[4,128,128]{2,1,0:T(8,128)(2,1)S(1)} %collective-permute-done.first_ref, bf16[4,128,128]{2,1,0:T(8,128)(2,1)S(1)} %collective-permute-done.1.second_ref, ...), custom_call_target="tpu_custom_call" | custom-call | tf_op jit(solution)/shard_map/unpack/pallas_call | solution.py:488
  16.6 3.3 %all-to-all-done = s32[16,1,4]{2,1,0:T(1,128)S(1)} async-done(((s32[16,1,4]{2,1,0:T(1,128)}), s32[16,1,4]{2,1,0:T(1,128)S(1)}, u32[]{:S(2)}, u32[]{:S(2)}) %all-to-all-start) | async-done | bytes 288 | tf_op jit(solution)/shard_map/all_to_all | solution.py:486
  20.0 0.0 copy-start.1
  20.0 0.0 copy-start.2
  20.0 1.2 %products.1 = f32[16,4,128]{2,1,0:T(4,128)S(1)} custom-call(s32[16,4]{1,0:T(8,128)S(1)} %bitcast.9, f32[16,2,2,4,8,128]{5,4,3,2,1,0:T(8,128)S(1)} %get-tuple-element.6.part_ref, f32[16,128]{1,0:T(8,128)S(1)} %get-tuple-element.7.root_ref, bf16[256,128]{1,0:T(8,128)(2,1)S(1)} %copy-done.3), custom_call_target="tpu_custom_call" | custom-call | tf_op jit(solution)/shard_map/products/pallas_call | solution.py:503
  21.2 0.0 copy-start.4
  21.2 0.0 copy-start.5
  21.2 9.9 %all_to_all.13.ratio_ref = f32[16,4,128]{2,1,0:T(4,128)S(1)} all-to-all(f32[16,4,128]{2,1,0:T(4,128)S(1)} %products.1), channel_id=1, replica_groups=mesh['tile'=2,'date'=4,'rng'=2,'az'=2] {'date','rng','az'}, dimensions={0} | all-to-all | bytes 65536 | tf_op jit(solution)/shard_map/all_to_all | solution.py:516
  31.2 0.0 copy-done
  31.2 0.0 copy-done.1
  31.2 0.0 copy-done.2
  31.2 0.0 copy-done.4
  31.2 0.0 copy-done.5
  31.2 1.9 %filter.1 = (bf16[2,2,32,64]{3,2,1,0:T(8,128)(2,1)}, bf16[2,32,64]{2,1,0:T(8,128)(2,1)}) custom-call(f32[16,4,128]{2,1,0:T(4,128)S(1)} %all_to_all.13.ratio_ref, bf16[1536,128]{1,0:T(8,128)(2,1)S(1)} %copy-done.1, bf16[32,256]{1,0:T(8,128)(2,1)S(1)} %copy-done.5, bf16[64,192]{1,0:T(8,128)(2,1)S(1)} %copy-done.4, bf16[256,768]{1,0:T(8,128)(2,1)S(1)} %copy-done.2, ...), custom_call_target="tpu_custom_call" | custom-call | tf_op jit(solution)/shard_map/filter/pallas_call | solution.py:526
Async XLA Ops:
  0.7 15.5 %copy-start.3 = (bf16[256,128]{1,0:T(8,128)(2,1)S(1)}, bf16[256,128]{1,0:T(8,128)(2,1)}, u32[]{:S(2)}) copy-start(bf16[256,128]{1,0:T(8,128)(2,1)} %constant.38.clone.window_ref) | copy-start | bytes 196612
  1.8 11.2 %collective-permute-start = (bf16[4,128,128]{2,1,0:T(8,128)(2,1)S(1)}, bf16[4,128,128]{2,1,0:T(8,128)(2,1)S(1)}, u32[]{:S(2)}, u32[]{:S(2)}) collective-permute-start(bf16[4,128,128]{2,1,0:T(8,128)(2,1)S(1)} %get-tuple-element.12), channel_id=1, source_target_pairs={{0,4},{1,5},{2,6},{3,7},{4,8},{5,9},{6,10},{7,11},{8,12},{9,13},{1... | collective-permute-start | bytes 393224 | tf_op jit(solution)/shard_map/ppermute | solution.py:480
  5.0 3.9 %copy-start.6 = (s32[2,2]{1,0:T(2,128)S(1)}, s32[2,2]{1,0:T(2,128)}, u32[]{:S(2)}) copy-start(s32[2,2]{1,0:T(2,128)} %param.9) | copy-start | bytes 52
  5.0 11.2 %collective-permute-start.1 = (bf16[4,128,128]{2,1,0:T(8,128)(2,1)S(1)}, bf16[4,128,128]{2,1,0:T(8,128)(2,1)S(1)}, u32[]{:S(2)}, u32[]{:S(2)}) collective-permute-start(bf16[4,128,128]{2,1,0:T(8,128)(2,1)S(1)} %get-tuple-element.11), channel_id=1, source_target_pairs={{0,8},{1,9},{2,10},{3,11},{4,12},{5,13},{6,14},{7,15},{8,0},{9,1},... | collective-permute-start | bytes 393224 | tf_op jit(solution)/shard_map/ppermute | solution.py:480
  7.5 8.6 %collective-permute-start.2 = (bf16[4,128,128]{2,1,0:T(8,128)(2,1)S(1)}, bf16[4,128,128]{2,1,0:T(8,128)(2,1)S(1)}, u32[]{:S(2)}, u32[]{:S(2)}) collective-permute-start(bf16[4,128,128]{2,1,0:T(8,128)(2,1)S(1)} %get-tuple-element.10), channel_id=1, source_target_pairs={{0,12},{1,13},{2,14},{3,15},{4,0},{5,1},{6,2},{7,3},{8,4},{9,5},{1... | collective-permute-start | bytes 393224 | tf_op jit(solution)/shard_map/ppermute | solution.py:480
  9.6 10.4 %all-to-all-start = ((s32[16,1,4]{2,1,0:T(1,128)}), s32[16,1,4]{2,1,0:T(1,128)S(1)}, u32[]{:S(2)}, u32[]{:S(2)}) async-start(s32[16,1,4]{2,1,0:T(1,128)} %broadcast_in_dim.8), calls=%async_computation | async-start | bytes 16384 | tf_op jit(solution)/shard_map/all_to_all | solution.py:486
  16.2 15.0 %copy-start = (bf16[1536,256]{1,0:T(8,128)(2,1)S(1)}, bf16[1536,256]{1,0:T(8,128)(2,1)}, u32[]{:S(2)}) copy-start(bf16[1536,256]{1,0:T(8,128)(2,1)} %constant.43.clone.end_ref) | copy-start | bytes 2359300
  20.0 11.2 %copy-start.1 = (bf16[1536,128]{1,0:T(8,128)(2,1)S(1)}, bf16[1536,128]{1,0:T(8,128)(2,1)}, u32[]{:S(2)}) copy-start(bf16[1536,128]{1,0:T(8,128)(2,1)} %constant.39.clone.sample_ref) | copy-start | bytes 1179652
  20.0 11.2 %copy-start.2 = (bf16[256,768]{1,0:T(8,128)(2,1)S(1)}, bf16[256,768]{1,0:T(8,128)(2,1)}, u32[]{:S(2)}) copy-start(bf16[256,768]{1,0:T(8,128)(2,1)} %constant.42.clone.back_ref) | copy-start | bytes 1179652
  21.2 10.0 %copy-start.4 = (bf16[64,192]{1,0:T(8,128)(2,1)S(1)}, bf16[64,192]{1,0:T(8,128)(2,1)}, u32[]{:S(2)}) copy-start(bf16[64,192]{1,0:T(8,128)(2,1)} %constant.41.clone.line_ref) | copy-start | bytes 73732
  21.2 10.0 %copy-start.5 = (bf16[32,256]{1,0:T(8,128)(2,1)S(1)}, bf16[32,256]{1,0:T(8,128)(2,1)}, u32[]{:S(2)}) copy-start(bf16[32,256]{1,0:T(8,128)(2,1)} %constant.40.clone.place_table_ref) | copy-start | bytes 49156
